TPU v7x, 128 devices: a whole 4x4x4 slice. The times are simulated.
128 devices in a mesh: ctx: 32 (over y, z, core), exp: 4 (over x).
Axes of the slice: x: 4, y: 4, z: 4, core: 2. Of those that a mesh axis runs over, the one named last changes fastest.
Arguments:
- stream_in: bfloat16 [4096, 6144], P('ctx'), may hold values from -41 to 41
- queries: bfloat16 [4096, 8192], P('ctx', 'exp'), may hold values from -6 to 6
- key_proj: bfloat16 [4096, 8192], P('ctx', 'exp'), may hold values from -0.5390625 to 0.5390625
- values: bfloat16 [4096, 8192], P('ctx', 'exp'), may hold values from -6 to 6
- attn_gate: bfloat16 [4096, 8192], P('ctx', 'exp'), may hold values from -6 to 6
- decay_rates: float32 [64], P('exp'), may hold values from 1.2207031e-05 to 0.05
- attn_gain: float32 [8192], P('exp'), may hold values from 0.25 to 1.75
- out_weight: bfloat16 [8192, 6144], P('exp', 'ctx'), may hold values from -0.0625 to 0.0625
- ffn_gain: float32 [6144], replicated, may hold values from 0.25 to 1.75
- routing: int32 [4096, 2], P('ctx'), may hold values from 0 to 31, as said below
- route_weights: float32 [4096, 2], P('ctx'), may hold values from 0.25 to 1
- w_gate: bfloat16 [4, 6144, 9216], P('exp', None, 'ctx'), may hold values from -0.078125 to 0.078125
- w_up: bfloat16 [4, 6144, 9216], P('exp', None, 'ctx'), may hold values from -0.078125 to 0.078125
- w_down: bfloat16 [4, 9216, 6144], P('exp', 'ctx'), may hold values from -0.0625 to 0.0625
Outputs:
- residual_out: bfloat16 [4096, 6144], P(('ctx', 'exp'))
- expert_out: bfloat16 [32, 4, 8, 6144], P('ctx', 'exp')
Inputs may be any that keep to these rules, and one draw needn't show every extreme that they name: `routing`: the two ids of a row differ and at most one of them is below 4. In each aligned block of 128 rows (one context shard) an id below 4 is named by at most 8 rows; one such id, the same for all blocks, is named by exactly 8 rows in every block.
All inputs are finite; a program needn't handle non-finite values.
Results may differ from a plain program's by a relative error of at most 0.025.
Values may be sent and summed in bfloat16 or wider, within the bound.
A program may use at most 128 MiB of HBM per device.

v0:
```python
import jax
import jax.numpy as jnp
from jax import lax
from jax.sharding import PartitionSpec as P

HIGHEST = lax.Precision.HIGHEST


def entering(value, axis, join, neutral):
    place = lax.axis_index(axis)
    gathered = jax.tree.map(
        lambda a, kind: lax.all_gather(a.astype(kind), axis), value, (jnp.bfloat16, jnp.bfloat16)
    )
    state = jax.tree.map(lambda a, e: jnp.zeros_like(a) + jnp.asarray(e, a.dtype), value, neutral)

    def one(step, state):
        return join(
            state,
            jax.tree.map(
                lambda a, own: lax.dynamic_index_in_dim(a, step, 0, False).astype(own.dtype),
                gathered,
                value,
            ),
        )

    return lax.fori_loop(0, place, one, state)


def normalize_rows(row_block, ffn_gain):
    wide_rows = row_block.astype(jnp.float32)
    inverse = lax.rsqrt(jnp.mean(wide_rows * wide_rows, axis=1, keepdims=True) + 1e-06)
    return (wide_rows * inverse * ffn_gain[None, :]).astype(jnp.bfloat16)


def prefix_combine(earlier_pair, later_pair):
    return (
        earlier_pair[0] * later_pair[0],
        later_pair[0][:, None, None] * earlier_pair[1] + later_pair[1],
    )


def per_device(
    stream_in,
    queries,
    key_proj,
    values,
    attn_gate,
    decay_rates,
    attn_gain,
    out_weight,
    ffn_gain,
    routing,
    route_weights,
    w_gate,
    w_up,
    w_down,
):
    rows_here, model_width = stream_in.shape
    head_count = decay_rates.shape[0]
    head_size = queries.shape[1] // head_count
    exp_count = lax.axis_size("exp")
    own_index = lax.axis_index("exp")
    capacity = rows_here // 16
    own_rows = rows_here // exp_count
    per_block = own_rows + capacity
    query_heads = queries.reshape(rows_here, head_count, head_size)
    key_heads = key_proj.reshape(rows_here, head_count, head_size)
    value_heads = values.reshape(rows_here, head_count, head_size)
    positions = jnp.arange(rows_here, dtype=jnp.float32)
    tail_decay = jnp.exp(-decay_rates[None, :] * (rows_here - 1.0 - positions)[:, None])
    weighted_keys = key_heads.astype(jnp.float32) * tail_decay[:, :, None]
    local_state = jnp.einsum(
        "jhd,jhe->hde", weighted_keys, value_heads.astype(jnp.float32), precision=HIGHEST
    )
    span_decay = jnp.exp(-decay_rates * rows_here)
    identity = (jnp.ones_like(span_decay), jnp.zeros_like(local_state))
    prefix_pair = entering((span_decay, local_state), "ctx", prefix_combine, identity)
    prior_state = prefix_pair[1]
    scores = jnp.einsum("ihd,jhd->hij", query_heads, key_heads, preferred_element_type=jnp.float32)
    distance = positions[:, None] - positions[None, :]
    decay_mask = jnp.where(
        distance[None] >= 0.0,
        jnp.exp(-decay_rates[:, None, None] * jnp.maximum(distance, 0.0)[None]),
        0.0,
    )
    near_weights = (scores * decay_mask).astype(jnp.bfloat16)
    near_part = jnp.einsum(
        "hij,jhd->ihd", near_weights, value_heads, preferred_element_type=jnp.float32
    )
    lead_decay = jnp.exp(-decay_rates[None, :] * (positions + 1.0)[:, None])
    far_part = jnp.einsum(
        "ihd,hde->ihe",
        query_heads.astype(jnp.float32) * lead_decay[:, :, None],
        prior_state,
        precision=HIGHEST,
    )
    attended = near_part + far_part
    inverse = lax.rsqrt(jnp.mean(attended * attended, axis=2, keepdims=True) + 1e-06)
    normed = (attended * inverse).reshape(rows_here, head_count * head_size)
    mixed_heads = (
        normed * attn_gain[None, :] * jax.nn.sigmoid(attn_gate.astype(jnp.float32))
    ).astype(jnp.bfloat16)
    held_ids = jnp.arange(exp_count, dtype=jnp.int32)
    hit_mask = routing[:, :, None] == held_ids[None, None, :]
    member = jnp.sum(hit_mask.astype(jnp.int32), axis=1)
    gate_of = jnp.sum(jnp.where(hit_mask, route_weights[:, :, None], 0.0), axis=1)
    slot_rank = jnp.cumsum(member, axis=0) - 1
    slot_index = jnp.arange(capacity, dtype=jnp.int32)
    pick_mask = (member[:, :, None] == 1) & (slot_rank[:, :, None] == slot_index[None, None, :])
    selector = pick_mask.reshape(rows_here, exp_count * capacity).T.astype(jnp.bfloat16)
    slot_weight = jnp.sum(jnp.where(pick_mask, gate_of[:, :, None], 0.0), axis=0)
    slot_mixed = jnp.dot(selector, mixed_heads, preferred_element_type=jnp.float32).astype(
        jnp.bfloat16
    )
    row_blocks = jnp.concatenate(
        [mixed_heads.reshape(exp_count, own_rows, -1), slot_mixed.reshape(exp_count, capacity, -1)],
        axis=1,
    )
    stacked = row_blocks.reshape(exp_count * per_block, head_count * head_size)
    partial_rows = jnp.dot(
        stacked,
        lax.all_gather(out_weight, "ctx", axis=1, tiled=True),
        preferred_element_type=jnp.float32,
    )
    partial_term = partial_rows.reshape(1, exp_count, per_block, model_width)
    summed = lax.psum_scatter(
        partial_term.astype(jnp.bfloat16), "exp", scatter_dimension=1, tiled=True
    ).astype(jnp.float32)
    projected = summed.reshape(per_block, model_width)
    stream_own = lax.dynamic_slice_in_dim(stream_in, own_index * own_rows, own_rows, 0)
    own_selector = lax.dynamic_slice_in_dim(selector, own_index * capacity, capacity, 0)
    stream_slots = jnp.dot(own_selector, stream_in, preferred_element_type=jnp.float32)
    residual_rows = jnp.concatenate([stream_own.astype(jnp.float32), stream_slots], axis=0)
    hidden_rows = (residual_rows + projected).astype(jnp.bfloat16)
    residual_out = hidden_rows[:own_rows]
    slot_hidden = hidden_rows[own_rows:]
    outgoing = normalize_rows(slot_hidden, ffn_gain)
    row_piece = lax.all_gather(outgoing, "ctx", axis=0, tiled=True)
    gate_part = jnp.dot(row_piece, w_gate[0], preferred_element_type=jnp.float32)
    up_part = jnp.dot(row_piece, w_up[0], preferred_element_type=jnp.float32)
    activated = (jax.nn.silu(gate_part) * up_part).astype(jnp.bfloat16)
    summed_down = lax.psum_scatter(
        jnp.dot(activated, w_down[0], preferred_element_type=jnp.float32).astype(jnp.bfloat16),
        "ctx",
        scatter_dimension=0,
        tiled=True,
    ).astype(jnp.float32)
    own_weight = lax.dynamic_index_in_dim(slot_weight, own_index, 0, keepdims=False)
    expert_out = (
        (summed_down * own_weight[:, None])
        .astype(jnp.bfloat16)
        .reshape(1, 1, capacity, model_width)
    )
    return (residual_out, expert_out)


def solution(mesh):
    return jax.shard_map(
        per_device,
        mesh=mesh,
        in_specs=(
            P("ctx", None),
            P("ctx", "exp"),
            P("ctx", "exp"),
            P("ctx", "exp"),
            P("ctx", "exp"),
            P("exp"),
            P("exp"),
            P("exp", "ctx"),
            P(),
            P("ctx", None),
            P("ctx", None),
            P("exp", None, "ctx"),
            P("exp", None, "ctx"),
            P("exp", "ctx", None),
        ),
        out_specs=(P(("ctx", "exp"), None), P("ctx", "exp", None, None)),
        check_vma=False,
    )
```

profile of v0, /device:TPU:0, one launch (start us, length us, event | category | flops | bytes accessed | tf_op | source)
XLA Modules:
  0.0 404.1 jit_solution(633874011973536907)
XLA Ops:
  7.7 1.5 exponential_convert_fusion
  9.2 2.0 copy.57
  12.0 2.7 convolution_convert_fusion.2
  18.3 70.0 %all-reduce = bf16[512]{0:T(512)(128)(2,1)S(1)} all-reduce(bf16[512]{0:T(512)(128)(2,1)S(1)} %dynamic-update-slice), channel_id=2, replica_groups=mesh['ctx'=32,'exp'=4] {'ctx'}, use_global_device_ids=true, to_apply=%add | all-reduce | flops 512 | bytes 2048
  90.4 1.6 reduce_window_sum.11
  92.0 1.5 broadcast_add_fusion
  98.1 3.1 convolution_bitcast_fusion.1
  102.3 4.2 %multiply_reduce_fusion = (f32[128,16]{0,1:T(8,128)S(1)}, f32[128,16,128]{0,2,1:T(8,128)S(1)}) fusion(f32[128,16,128]{0,2,1:T(8,128)} %convolution_bitcast_fusion.1, f32[16,128,128]{2,1,0:T(8,128)} %get-tuple-element.46, f32[128,16]{0,1:T(8,128)S(1)} %get-tuple-element.57, bf16[128,2048]{1,0:T(8,128)(2,1)} %param.17), kind=kOutput, calls=%fused_computation.23 | convolution fusion | flops 403961856 | bytes 3686400 | tf_op jit(solution)/shard_map/ihd,hde->ihe/dot_general | solution.py:91
  107.7 2.5 copy.55
  110.2 1.7 multiply_convert_fusion
  112.7 1.5 fusion.13
  114.3 69.8 %all-gather.6.cloned.1.call-done = bf16[2048,6144]{0,1:T(8,128)(2,1)} async-done(((bf16[2048,192]{0,1:T(8,128)(2,1)}), bf16[2048,6144]{0,1:T(8,128)(2,1)}) %all-gather.6.cloned.1.call-update) | async-done | bytes 25165840 | tf_op jit(solution)/shard_map/all_gather | solution.py:122
  184.1 14.1 %fusion.5 = bf16[1,4,40,6144]{3,2,1,0:T(8,128)(2,1)} fusion(bf16[2048,6144]{0,1:T(8,128)(2,1)} %all-gather.6.cloned.1.call-done, bf16[4,8,2048]{2,1,0:T(8,128)(2,1)} %fusion.13, bf16[4,32,2048]{2,1,0:T(8,128)(2,1)} %bitcast.101), kind=kOutput, calls=%fused_computation.6 | convolution fusion | flops 4028825600 | bytes 27787264 | tf_op jit(solution)/shard_map/dot_general | solution.py:120
  198.4 2.4 fusion.65
  200.8 1.9 dynamic-slice_convert_fusion
  202.7 50.3 %reduce-scatter.3.cloned.1.call-done = bf16[1,1,40,6144]{3,2,1,0:T(8,128)(2,1)} async-done(((bf16[1,4,40,6144]{3,2,1,0:T(8,128)(2,1)}), bf16[1,1,40,6144]{3,2,1,0:T(8,128)(2,1)}) %reduce-scatter.3.cloned.1.call-update) | async-done | bytes 491536 | tf_op jit(solution)/shard_map/reduce_scatter | solution.py:126
  253.0 1.4 fusion.29
  255.2 1.5 fusion.58
  256.9 44.9 %all-gather.8.cloned.1.call-done = bf16[256,6144]{1,0:T(8,128)(2,1)} async-done(((bf16[8,6144]{1,0:T(8,128)(2,1)}), bf16[256,6144]{1,0:T(8,128)(2,1)}) %all-gather.8.cloned.1.call-update) | async-done | bytes 3145744 | tf_op jit(solution)/shard_map/all_gather | solution.py:138
  301.8 4.8 %fusion.11 = f32[256,288]{0,1:T(8,128)} fusion(bf16[256,6144]{1,0:T(8,128)(2,1)} %all-gather.8.cloned.1.call-done, bf16[1,6144,288]{1,2,0:T(8,128)(2,1)} %param.27), kind=kOutput, calls=%fused_computation.10 | convolution fusion | flops 905969664 | bytes 6979584 | tf_op jit(solution)/shard_map/dot_general | solution.py:139
  306.6 9.4 %convolution_convert_fusion = bf16[256,6144]{1,0:T(8,128)(2,1)} fusion(bf16[1,288,6144]{2,1,0:T(8,128)(2,1)S(1)} %copy-done, bf16[256,6144]{1,0:T(8,128)(2,1)} %all-gather.8.cloned.1.call-done, bf16[1,6144,288]{1,2,0:T(8,128)(2,1)} %param.28, f32[256,288]{0,1:T(8,128)} %fusion.11), kind=kOutput, calls=%fused_computation.4 | convolution fusion | flops 1813954560 | bytes 13664256 | tf_op jit(solution)/shard_map/dot_general | solution.py:143
  316.2 1.8 slice.8
  318.0 78.0 %reduce-scatter.5.cloned.1.call-done = bf16[8,6144]{1,0:T(8,128)(2,1)} async-done(((bf16[256,6144]{1,0:T(8,128)(2,1)}), bf16[8,6144]{1,0:T(8,128)(2,1)}) %reduce-scatter.5.cloned.1.call-update) | async-done | bytes 98320 | tf_op jit(solution)/shard_map/reduce_scatter | solution.py:142
  396.0 1.6 fusion.60
  (53 shorter events, 15.4 us)
Async XLA Ops:
  7.2 299.5 %copy-start = (bf16[1,288,6144]{2,1,0:T(8,128)(2,1)S(1)}, bf16[1,288,6144]{2,1,0:T(8,128)(2,1)}, u32[]{:S(2)}) copy-start(bf16[1,288,6144]{2,1,0:T(8,128)(2,1)} %param.29) | copy-start | bytes 10616836
  7.2 94.0 %all-gather.10.cloned.1.call-start = ((), (), s32[]{:S(2)}) async-start(), calls=%async_computation.6 | async-start | bytes 17301504 | tf_op jit(solution)/shard_map/all_gather | solution.py:12
  9.2 8.2 %copy-start.8 = (f32[16]{0:T(128)}, f32[16]{0:T(128)S(1)}, u32[]{:S(2)}) copy-start(f32[16]{0:T(128)S(1)} %get-tuple-element.60) | copy-start | bytes 196
  14.7 169.4 %all-gather.6.cloned.1.call-start = ((), (), s32[]{:S(2)}) async-start(), calls=%async_computation.2 | async-start | bytes 25952256 | tf_op jit(solution)/shard_map/all_gather | solution.py:122
  15.4 237.6 %reduce-scatter.3.cloned.1.call-start = ((), (), s32[]{:S(2)}) async-start(), calls=%async_computation.3 | async-start | bytes 2457600 | tf_op jit(solution)/shard_map/reduce_scatter | solution.py:126
  106.5 3.7 copy-start.3
  106.5 6.2 %copy-start.4 = (pred[128,4]{0,1:T(4,128)(4,1)S(1)}, pred[128,4]{0,1:T(4,128)(4,1)}, u32[]{:S(2)}) copy-start(pred[128,4]{0,1:T(4,128)(4,1)} %broadcast_compare_fusion) | copy-start | bytes 1540
  111.9 0.8 copy-start.2
  184.1 14.2 %copy-start.5 = (s32[32]{0:T(128)S(1)}, s32[32]{0:T(128)}, u32[]{:S(2)}) copy-start(s32[32]{0:T(128)} %eq.56) | copy-start | bytes 388
  198.3 103.6 %all-gather.8.cloned.1.call-start = ((), (), s32[]{:S(2)}) async-start(), calls=%async_computation.4 | async-start | bytes 3244032 | tf_op jit(solution)/shard_map/all_gather | solution.py:138
  254.4 0.8 copy-start.1
  256.7 139.3 %reduce-scatter.5.cloned.1.call-start = ((), (), s32[]{:S(2)}) async-start(), calls=%async_computation.5 | async-start | bytes 3244032 | tf_op jit(solution)/shard_map/reduce_scatter | solution.py:142
  306.6 9.4 %copy-start.6 = (s32[128,2]{0,1:T(2,128)S(1)}, s32[128,2]{0,1:T(2,128)}, u32[]{:S(2)}) copy-start(s32[128,2]{0,1:T(2,128)} %param.25) | copy-start | bytes 3076
  306.6 9.4 %copy-start.7 = (f32[128,2]{0,1:T(2,128)S(1)}, f32[128,2]{0,1:T(2,128)}, u32[]{:S(2)}) copy-start(f32[128,2]{0,1:T(2,128)} %param.26) | copy-start | bytes 3076
Sparse Core Ops, SparseCore 0:
  14.8 75.4 all-gather.9
  92.6 91.4 all-gather.5
  198.4 54.6 reduce-scatter.2
  256.8 44.9 all-gather.7
  316.2 79.7 reduce-scatter.4
where the time goes:
time: 406 us; the launch traced here: 404 us
  waiting for transfers between devices  244 us (60%)
  blocking collectives  70 us (17%)
  matrix products  42.2 us (10%)
  other arithmetic  18 us (4%)
  local copies, waits for them, and re-layouts  15.3 us (4%)
  between operations  14.6 us (4%)
    reduce_scatter x1, waiting for transfers between devices, per_device(): lax.psum_scatter(jnp.dot(activated, w_down[0], preferred_element_type=jnp...  78 us
    unnamed x1, blocking collectives  70 us
    all_gather x1, waiting for transfers between devices, per_device(): lax.all_gather(out_weight, 'ctx', axis=1, tiled=True)  69.8 us
    reduce_scatter x1, waiting for transfers between devices, per_device(): lax.psum_scatter(partial_term.astype(jnp.bfloat16), 'exp', scatter_dimens...  50.3 us
    all_gather x1, waiting for transfers between devices, per_device(): row_piece = lax.all_gather(outgoing, 'ctx', axis=0, tiled=True)  44.9 us
    dot_general x1, matrix products, per_device(): jnp.dot(stacked, lax.all_gather(out_weight, 'ctx', axis=1, tiled=True), p...  14.1 us
    dot_general x1, matrix products, per_device(): jnp.dot(activated, w_down[0], preferred_element_type=jnp.float32)  9.41 us
  transfers between devices with their start and end apart: 5, of which 4 were waited for; matrix products, arithmetic and copies ran while one was open for 8% of the time, Pallas kernels for 0%

commit v1 on v0

--- a/solution.py
+++ b/solution.py
@@ -6,37 +6,26 @@
 HIGHEST = lax.Precision.HIGHEST
 
 
-def entering(value, axis, join, neutral):
-    place = lax.axis_index(axis)
-    gathered = jax.tree.map(
-        lambda a, kind: lax.all_gather(a.astype(kind), axis), value, (jnp.bfloat16, jnp.bfloat16)
-    )
-    state = jax.tree.map(lambda a, e: jnp.zeros_like(a) + jnp.asarray(e, a.dtype), value, neutral)
+def decayed_prefix(local_state, decay_rates, rows_here):
+    count = lax.axis_size("ctx")
 
-    def one(step, state):
-        return join(
-            state,
-            jax.tree.map(
-                lambda a, own: lax.dynamic_index_in_dim(a, step, 0, False).astype(own.dtype),
-                gathered,
-                value,
-            ),
-        )
+    def shift(value, step):
+        pairs = [(i, i + step) for i in range(count - step)]
+        return lax.ppermute(value.astype(jnp.bfloat16), "ctx", pairs).astype(jnp.float32)
 
-    return lax.fori_loop(0, place, one, state)
+    running = shift(local_state, 1)
+    step = 1
+    while step < count:
+        factor = jnp.exp(-decay_rates * (rows_here * step))
+        running = running + factor[:, None, None] * shift(running, step)
+        step *= 2
+    return running
 
 
 def normalize_rows(row_block, ffn_gain):
     wide_rows = row_block.astype(jnp.float32)
     inverse = lax.rsqrt(jnp.mean(wide_rows * wide_rows, axis=1, keepdims=True) + 1e-06)
     return (wide_rows * inverse * ffn_gain[None, :]).astype(jnp.bfloat16)
-
-
-def prefix_combine(earlier_pair, later_pair):
-    return (
-        earlier_pair[0] * later_pair[0],
-        later_pair[0][:, None, None] * earlier_pair[1] + later_pair[1],
-    )
 
 
 def per_device(
@@ -72,10 +61,7 @@
     local_state = jnp.einsum(
         "jhd,jhe->hde", weighted_keys, value_heads.astype(jnp.float32), precision=HIGHEST
     )
-    span_decay = jnp.exp(-decay_rates * rows_here)
-    identity = (jnp.ones_like(span_decay), jnp.zeros_like(local_state))
-    prefix_pair = entering((span_decay, local_state), "ctx", prefix_combine, identity)
-    prior_state = prefix_pair[1]
+    prior_state = decayed_prefix(local_state, decay_rates, rows_here)
     scores = jnp.einsum("ihd,jhd->hij", query_heads, key_heads, preferred_element_type=jnp.float32)
     distance = positions[:, None] - positions[None, :]
     decay_mask = jnp.where(

time: 406 us -> 352 us (0.87)
  blocking collectives: 70 us -> 0 us
  starting transfers between devices: 0.38 us -> 63.2 us
  waiting for transfers between devices: 244 us -> 198 us
    unnamed x1 -> x0, blocking collectives: 70 us -> none
    all_gather x1, waiting for transfers between devices: 69.8 us -> 0.01 us  [per_device(): lax.all_gather(out_weight, 'ctx', axis=1, tiled=True)]
    ppermute x0 -> x6, starting transfers between devices: none -> 62.9 us  [shift(): lax.ppermute(value.astype(jnp.bfloat16), 'ctx', pairs).astype(jnp.float32)]
    ppermute x0 -> x6, waiting for transfers between devices: none -> 48 us  [shift(): lax.ppermute(value.astype(jnp.bfloat16), 'ctx', pairs).astype(jnp.float32)]
    reduce_scatter x1, waiting for transfers between devices: 50.3 us -> 26.9 us  [per_device(): lax.psum_scatter(partial_term.astype(jnp.bfloat16), 'exp', scatter_dimens...]
  transfers between devices with their start and end apart: 5 -> 10, of which waited for: 4 -> 8; matrix products, arithmetic and copies ran while one was open for 8% -> 12% of each run, Pallas kernels for 0% -> 0%
where the time goes in v1:
time: 352 us; the launch traced here: 351 us
  waiting for transfers between devices  198 us (56%)
  starting transfers between devices  63.2 us (18%)
  matrix products  42.3 us (12%)
  other arithmetic  21 us (6%)
  between operations  13.9 us (4%)
  local copies, waits for them, and re-layouts  12.3 us (3%)
    reduce_scatter x1, waiting for transfers between devices, per_device(): lax.psum_scatter(jnp.dot(activated, w_down[0], preferred_element_type=jnp...  77.4 us
    ppermute x6, starting transfers between devices, shift(): lax.ppermute(value.astype(jnp.bfloat16), 'ctx', pairs).astype(jnp.float32)  62.9 us
    ppermute x6, waiting for transfers between devices, shift(): lax.ppermute(value.astype(jnp.bfloat16), 'ctx', pairs).astype(jnp.float32)  48 us
    all_gather x1, waiting for transfers between devices, per_device(): row_piece = lax.all_gather(outgoing, 'ctx', axis=0, tiled=True)  45.1 us
    reduce_scatter x1, waiting for transfers between devices, per_device(): lax.psum_scatter(partial_term.astype(jnp.bfloat16), 'exp', scatter_dimens...  26.9 us
    dot_general x1, matrix products, per_device(): jnp.dot(stacked, lax.all_gather(out_weight, 'ctx', axis=1, tiled=True), p...  14.1 us
    dot_general x1, matrix products, per_device(): jnp.dot(activated, w_down[0], preferred_element_type=jnp.float32)  9.38 us
  transfers between devices with their start and end apart: 10, of which 8 were waited for; matrix products, arithmetic and copies ran while one was open for 12% of the time, Pallas kernels for 0%

profile of v1, /device:TPU:0, one launch (start us, length us, event | category | flops | bytes accessed | tf_op | source)
XLA Modules:
  0.0 350.8 jit_solution(12923817143671635209)
XLA Ops:
  8.0 2.3 copy.45
  11.6 1.9 convolution_convert_fusion.2
  16.3 9.2 %collective-permute-start.1 = (bf16[16,128,128]{2,1,0:T(8,128)(2,1)S(1)}, bf16[16,128,128]{2,1,0:T(8,128)(2,1)S(1)}, u32[]{:S(2)}, u32[]{:S(2)}) collective-permute-start(bf16[16,128,128]{2,1,0:T(8,128)(2,1)S(1)} %collective-permute-done), channel_id=1, source_target_pairs={{0,4},{4,8},{8,12},{12,16},{16,20},{20,24},{24,28},{28,32},{32,36}... | collective-permute-start | bytes 1572872 | tf_op jit(solution)/shard_map/ppermute | solution.py:14
  27.4 19.8 %collective-permute-start.2 = (bf16[16,128,128]{2,1,0:T(8,128)(2,1)S(1)}, bf16[16,128,128]{2,1,0:T(8,128)(2,1)S(1)}, u32[]{:S(2)}, u32[]{:S(2)}) collective-permute-start(bf16[16,128,128]{2,1,0:T(8,128)(2,1)S(1)} %fusion.33), channel_id=1, source_target_pairs={{0,8},{4,12},{8,16},{12,20},{16,24},{20,28},{24,32},{28,36},{32,40... | collective-permute-start | bytes 1572872 | tf_op jit(solution)/shard_map/ppermute | solution.py:14
  47.2 17.4 %collective-permute-done.2 = bf16[16,128,128]{2,1,0:T(8,128)(2,1)S(1)} collective-permute-done((bf16[16,128,128]{2,1,0:T(8,128)(2,1)S(1)}, bf16[16,128,128]{2,1,0:T(8,128)(2,1)S(1)}, u32[]{:S(2)}, u32[]{:S(2)}) %collective-permute-start.2) | collective-permute-done | bytes 524320 | tf_op jit(solution)/shard_map/ppermute | solution.py:14
  65.0 5.9 %collective-permute-start.3 = (bf16[16,128,128]{2,1,0:T(8,128)(2,1)S(1)}, bf16[16,128,128]{2,1,0:T(8,128)(2,1)S(1)}, u32[]{:S(2)}, u32[]{:S(2)}) collective-permute-start(bf16[16,128,128]{2,1,0:T(8,128)(2,1)S(1)} %fusion.80), channel_id=1, source_target_pairs={{0,16},{4,20},{8,24},{12,28},{16,32},{20,36},{24,40},{28,44},{32,4... | collective-permute-start | bytes 1572872 | tf_op jit(solution)/shard_map/ppermute | solution.py:14
  70.9 21.4 %collective-permute-done.3 = bf16[16,128,128]{2,1,0:T(8,128)(2,1)S(1)} collective-permute-done((bf16[16,128,128]{2,1,0:T(8,128)(2,1)S(1)}, bf16[16,128,128]{2,1,0:T(8,128)(2,1)S(1)}, u32[]{:S(2)}, u32[]{:S(2)}) %collective-permute-start.3) | collective-permute-done | bytes 524320 | tf_op jit(solution)/shard_map/ppermute | solution.py:14
  93.6 10.1 %collective-permute-start.4 = (bf16[16,128,128]{2,1,0:T(8,128)(2,1)}, bf16[16,128,128]{2,1,0:T(8,128)(2,1)}, u32[]{:S(2)}, u32[]{:S(2)}) collective-permute-start(bf16[16,128,128]{2,1,0:T(8,128)(2,1)} %fusion.36), channel_id=1, source_target_pairs={{0,32},{4,36},{8,40},{12,44},{16,48},{20,52},{24,56},{28,60},{32,6... | collective-permute-start | bytes 1572872 | tf_op jit(solution)/shard_map/ppermute | solution.py:14
  108.2 6.3 %collective-permute-done.4 = bf16[16,128,128]{2,1,0:T(8,128)(2,1)} collective-permute-done((bf16[16,128,128]{2,1,0:T(8,128)(2,1)}, bf16[16,128,128]{2,1,0:T(8,128)(2,1)}, u32[]{:S(2)}, u32[]{:S(2)}) %collective-permute-start.4) | collective-permute-done | bytes 524320 | tf_op jit(solution)/shard_map/ppermute | solution.py:14
  114.5 3.1 fusion.79
  117.6 16.5 %collective-permute-start.5 = (bf16[16,128,128]{2,1,0:T(8,128)(2,1)}, bf16[16,128,128]{2,1,0:T(8,128)(2,1)}, u32[]{:S(2)}, u32[]{:S(2)}) collective-permute-start(bf16[16,128,128]{2,1,0:T(8,128)(2,1)} %fusion.79), channel_id=1, source_target_pairs={{0,64},{4,68},{8,72},{12,76},{16,80},{20,84},{24,88},{28,92},{32,9... | collective-permute-start | bytes 1572872 | tf_op jit(solution)/shard_map/ppermute | solution.py:14
  138.0 3.2 convolution_bitcast_fusion.1
  141.2 5.1 %multiply_reduce_fusion = (f32[128,16]{0,1:T(8,128)S(1)}, f32[128,16,128]{0,2,1:T(8,128)S(1)}) fusion(f32[128,16,128]{0,2,1:T(8,128)} %convolution_bitcast_fusion.1, f32[128,16]{0,1:T(8,128)S(1)} %get-tuple-element.8, bf16[16,128,128]{2,1,0:T(8,128)(2,1)} %collective-permute-done.5, f32[16]{0:T(128)} %get-tuple-element.2, ...), kind=kOutput, calls=%fused_computation.21 | convolution fusion | flops 408156160 | bytes 5783872 | tf_op jit(solution)/shard_map/ihd,hde->ihe/dot_general | solution.py:77
  147.5 2.5 copy.43
  150.0 1.7 multiply_convert_fusion
  154.0 14.1 %fusion.5 = bf16[1,4,40,6144]{3,2,1,0:T(8,128)(2,1)} fusion(bf16[2048,6144]{0,1:T(8,128)(2,1)} %all-gather.3.cloned.1.call-done, bf16[4,8,2048]{2,1,0:T(8,128)(2,1)} %fusion.13, bf16[4,32,2048]{2,1,0:T(8,128)(2,1)} %bitcast.88), kind=kOutput, calls=%fused_computation.4 | convolution fusion | flops 4028825600 | bytes 27787264 | tf_op jit(solution)/shard_map/dot_general | solution.py:106
  168.5 2.4 fusion.71
  170.9 2.0 dynamic-slice_convert_fusion
  172.8 26.9 %reduce-scatter.3.cloned.1.call-done = bf16[1,1,40,6144]{3,2,1,0:T(8,128)(2,1)} async-done(((bf16[1,4,40,6144]{3,2,1,0:T(8,128)(2,1)}), bf16[1,1,40,6144]{3,2,1,0:T(8,128)(2,1)}) %reduce-scatter.3.cloned.1.call-update) | async-done | bytes 491536 | tf_op jit(solution)/shard_map/reduce_scatter | solution.py:112
  203.5 45.1 %all-gather.5.cloned.1.call-done = bf16[256,6144]{1,0:T(8,128)(2,1)} async-done(((bf16[8,6144]{1,0:T(8,128)(2,1)}), bf16[256,6144]{1,0:T(8,128)(2,1)}) %all-gather.5.cloned.1.call-update) | async-done | bytes 3145744 | tf_op jit(solution)/shard_map/all_gather | solution.py:124
  248.5 4.8 %fusion.11 = f32[256,288]{0,1:T(8,128)} fusion(bf16[256,6144]{1,0:T(8,128)(2,1)} %all-gather.5.cloned.1.call-done, bf16[1,6144,288]{1,2,0:T(8,128)(2,1)} %param.25), kind=kOutput, calls=%fused_computation.8 | convolution fusion | flops 905969664 | bytes 6979584 | tf_op jit(solution)/shard_map/dot_general | solution.py:125
  253.3 9.4 %convolution_convert_fusion = bf16[256,6144]{1,0:T(8,128)(2,1)} fusion(bf16[1,288,6144]{2,1,0:T(8,128)(2,1)S(1)} %copy-done, bf16[256,6144]{1,0:T(8,128)(2,1)} %all-gather.5.cloned.1.call-done, bf16[1,6144,288]{1,2,0:T(8,128)(2,1)} %param.26, f32[256,288]{0,1:T(8,128)} %fusion.11), kind=kOutput, calls=%fused_computation.2 | convolution fusion | flops 1813954560 | bytes 13664256 | tf_op jit(solution)/shard_map/dot_general | solution.py:129
  263.5 1.8 slice.8
  265.3 77.4 %reduce-scatter.5.cloned.1.call-done = bf16[8,6144]{1,0:T(8,128)(2,1)} async-done(((bf16[256,6144]{1,0:T(8,128)(2,1)}), bf16[8,6144]{1,0:T(8,128)(2,1)}) %reduce-scatter.5.cloned.1.call-update) | async-done | bytes 98320 | tf_op jit(solution)/shard_map/reduce_scatter | solution.py:128
  (75 shorter events, 26.8 us)
Async XLA Ops:
  7.2 246.1 %copy-start = (bf16[1,288,6144]{2,1,0:T(8,128)(2,1)S(1)}, bf16[1,288,6144]{2,1,0:T(8,128)(2,1)}, u32[]{:S(2)}) copy-start(bf16[1,288,6144]{2,1,0:T(8,128)(2,1)} %param.27) | copy-start | bytes 10616836
  7.2 146.8 %all-gather.3.cloned.1.call-start = ((), (), s32[]{:S(2)}) async-start(), calls=%async_computation.2 | async-start | bytes 25952256 | tf_op jit(solution)/shard_map/all_gather | solution.py:108
  7.9 191.8 %reduce-scatter.3.cloned.1.call-start = ((), (), s32[]{:S(2)}) async-start(), calls=%async_computation.3 | async-start | bytes 2457600 | tf_op jit(solution)/shard_map/reduce_scatter | solution.py:112
  11.5 80.7 %copy-start.15 = (f32[16]{0:T(128)}, f32[16]{0:T(128)S(1)}, u32[]{:S(2)}) copy-start(f32[16]{0:T(128)S(1)} %get-tuple-element.7) | copy-start | bytes 196
  11.5 82.1 %copy-start.8 = (f32[16]{0:T(128)}, f32[16]{0:T(128)S(1)}, u32[]{:S(2)}) copy-start(f32[16]{0:T(128)S(1)} %get-tuple-element.4) | copy-start | bytes 196
  11.5 82.1 %copy-start.11 = (f32[16]{0:T(128)}, f32[16]{0:T(128)S(1)}, u32[]{:S(2)}) copy-start(f32[16]{0:T(128)S(1)} %get-tuple-element.5) | copy-start | bytes 196
  11.6 103.0 %copy-start.7 = (f32[16]{0:T(128)}, f32[16]{0:T(128)S(1)}, u32[]{:S(2)}) copy-start(f32[16]{0:T(128)S(1)} %get-tuple-element.3) | copy-start | bytes 196
  13.5 2.8 collective-permute-start
  16.3 77.3 %copy-start.1 = (bf16[16,128,128]{2,1,0:T(8,128)(2,1)}, bf16[16,128,128]{2,1,0:T(8,128)(2,1)S(1)}, u32[]{:S(2)}) copy-start(bf16[16,128,128]{2,1,0:T(8,128)(2,1)S(1)} %collective-permute-done) | copy-start | bytes 1572868
  16.3 10.7 %collective-permute-start.1 = (bf16[16,128,128]{2,1,0:T(8,128)(2,1)S(1)}, bf16[16,128,128]{2,1,0:T(8,128)(2,1)S(1)}, u32[]{:S(2)}, u32[]{:S(2)}) collective-permute-start(bf16[16,128,128]{2,1,0:T(8,128)(2,1)S(1)} %collective-permute-done), channel_id=1, source_target_pairs={{0,4},{4,8},{8,12},{12,16},{16,20},{20,24},{24,28},{28,32},{32,36}... | collective-permute-start | bytes 1572872 | tf_op jit(solution)/shard_map/ppermute | solution.py:14
  27.1 66.6 %copy-start.2 = (bf16[16,128,128]{2,1,0:T(8,128)(2,1)}, bf16[16,128,128]{2,1,0:T(8,128)(2,1)S(1)}, u32[]{:S(2)}) copy-start(bf16[16,128,128]{2,1,0:T(8,128)(2,1)S(1)} %collective-permute-done.1) | copy-start | bytes 1572868
  27.1 76.6 %copy-start.13 = (s32[128,2]{0,1:T(2,128)S(1)}, s32[128,2]{0,1:T(2,128)}, u32[]{:S(2)}) copy-start(s32[128,2]{0,1:T(2,128)} %param.23) | copy-start | bytes 3076
  27.4 37.2 %collective-permute-start.2 = (bf16[16,128,128]{2,1,0:T(8,128)(2,1)S(1)}, bf16[16,128,128]{2,1,0:T(8,128)(2,1)S(1)}, u32[]{:S(2)}, u32[]{:S(2)}) collective-permute-start(bf16[16,128,128]{2,1,0:T(8,128)(2,1)S(1)} %fusion.33), channel_id=1, source_target_pairs={{0,8},{4,12},{8,16},{12,20},{16,24},{20,28},{24,32},{28,36},{32,40... | collective-permute-start | bytes 1572872 | tf_op jit(solution)/shard_map/ppermute | solution.py:14
  64.6 39.2 %copy-start.3 = (bf16[16,128,128]{2,1,0:T(8,128)(2,1)}, bf16[16,128,128]{2,1,0:T(8,128)(2,1)S(1)}, u32[]{:S(2)}) copy-start(bf16[16,128,128]{2,1,0:T(8,128)(2,1)S(1)} %collective-permute-done.2) | copy-start | bytes 1572868
  65.0 27.3 %collective-permute-start.3 = (bf16[16,128,128]{2,1,0:T(8,128)(2,1)S(1)}, bf16[16,128,128]{2,1,0:T(8,128)(2,1)S(1)}, u32[]{:S(2)}, u32[]{:S(2)}) collective-permute-start(bf16[16,128,128]{2,1,0:T(8,128)(2,1)S(1)} %fusion.80), channel_id=1, source_target_pairs={{0,16},{4,20},{8,24},{12,28},{16,32},{20,36},{24,40},{28,44},{32,4... | collective-permute-start | bytes 1572872 | tf_op jit(solution)/shard_map/ppermute | solution.py:14
  92.3 11.4 %copy-start.4 = (bf16[16,128,128]{2,1,0:T(8,128)(2,1)}, bf16[16,128,128]{2,1,0:T(8,128)(2,1)S(1)}, u32[]{:S(2)}) copy-start(bf16[16,128,128]{2,1,0:T(8,128)(2,1)S(1)} %collective-permute-done.3) | copy-start | bytes 1572868
  93.6 20.9 %collective-permute-start.4 = (bf16[16,128,128]{2,1,0:T(8,128)(2,1)}, bf16[16,128,128]{2,1,0:T(8,128)(2,1)}, u32[]{:S(2)}, u32[]{:S(2)}) collective-permute-start(bf16[16,128,128]{2,1,0:T(8,128)(2,1)} %fusion.36), channel_id=1, source_target_pairs={{0,32},{4,36},{8,40},{12,44},{16,48},{20,52},{24,56},{28,60},{32,6... | collective-permute-start | bytes 1572872 | tf_op jit(solution)/shard_map/ppermute | solution.py:14
  117.6 23.6 %collective-permute-start.5 = (bf16[16,128,128]{2,1,0:T(8,128)(2,1)}, bf16[16,128,128]{2,1,0:T(8,128)(2,1)}, u32[]{:S(2)}, u32[]{:S(2)}) collective-permute-start(bf16[16,128,128]{2,1,0:T(8,128)(2,1)} %fusion.79), channel_id=1, source_target_pairs={{0,64},{4,68},{8,72},{12,76},{16,80},{20,84},{24,88},{28,92},{32,9... | collective-permute-start | bytes 1572872 | tf_op jit(solution)/shard_map/ppermute | solution.py:14
  146.3 3.7 %copy-start.9 = (f32[2048]{0:T(1024)S(1)}, f32[2048]{0:T(1024)}, u32[]{:S(2)}) copy-start(f32[2048]{0:T(1024)} %param.20) | copy-start | bytes 24580
  146.3 6.2 %copy-start.10 = (pred[128,4]{0,1:T(4,128)(4,1)S(1)}, pred[128,4]{0,1:T(4,128)(4,1)}, u32[]{:S(2)}) copy-start(pred[128,4]{0,1:T(4,128)(4,1)} %broadcast_compare_fusion) | copy-start | bytes 1540
  151.7 0.8 copy-start.6
  154.0 14.4 %copy-start.12 = (s32[32]{0:T(128)S(1)}, s32[32]{0:T(128)}, u32[]{:S(2)}) copy-start(s32[32]{0:T(128)} %eq.56) | copy-start | bytes 388
  168.2 80.4 %all-gather.5.cloned.1.call-start = ((), (), s32[]{:S(2)}) async-start(), calls=%async_computation.4 | async-start | bytes 3244032 | tf_op jit(solution)/shard_map/all_gather | solution.py:124
  203.4 139.3 %reduce-scatter.5.cloned.1.call-start = ((), (), s32[]{:S(2)}) async-start(), calls=%async_computation.5 | async-start | bytes 3244032 | tf_op jit(solution)/shard_map/reduce_scatter | solution.py:128
  (3 other events, 2.2 us)
Sparse Core Ops, SparseCore 0:
  10.3 109.4 all-gather.2
  168.3 31.3 reduce-scatter.2
  203.5 44.9 all-gather.4
  262.8 79.7 reduce-scatter.4

commit v2 on v1

--- a/solution.py
+++ b/solution.py
@@ -109,10 +109,10 @@
         preferred_element_type=jnp.float32,
     )
     partial_term = partial_rows.reshape(1, exp_count, per_block, model_width)
-    summed = lax.psum_scatter(
-        partial_term.astype(jnp.bfloat16), "exp", scatter_dimension=1, tiled=True
-    ).astype(jnp.float32)
-    projected = summed.reshape(per_block, model_width)
+    swapped = lax.all_to_all(
+        partial_term.astype(jnp.bfloat16), "exp", 1, 0, tiled=True
+    )
+    projected = jnp.sum(swapped.astype(jnp.float32), axis=0).reshape(per_block, model_width)
     stream_own = lax.dynamic_slice_in_dim(stream_in, own_index * own_rows, own_rows, 0)
     own_selector = lax.dynamic_slice_in_dim(selector, own_index * capacity, capacity, 0)
     stream_slots = jnp.dot(own_selector, stream_in, preferred_element_type=jnp.float32)
@@ -121,16 +121,18 @@
     residual_out = hidden_rows[:own_rows]
     slot_hidden = hidden_rows[own_rows:]
     outgoing = normalize_rows(slot_hidden, ffn_gain)
-    row_piece = lax.all_gather(outgoing, "ctx", axis=0, tiled=True)
+    ctx_count = lax.axis_size("ctx")
+    row_piece = lax.all_to_all(
+        jnp.broadcast_to(outgoing[None], (ctx_count,) + outgoing.shape), "ctx", 0, 0, tiled=True
+    ).reshape(ctx_count * capacity, model_width)
     gate_part = jnp.dot(row_piece, w_gate[0], preferred_element_type=jnp.float32)
     up_part = jnp.dot(row_piece, w_up[0], preferred_element_type=jnp.float32)
     activated = (jax.nn.silu(gate_part) * up_part).astype(jnp.bfloat16)
-    summed_down = lax.psum_scatter(
-        jnp.dot(activated, w_down[0], preferred_element_type=jnp.float32).astype(jnp.bfloat16),
-        "ctx",
-        scatter_dimension=0,
-        tiled=True,
-    ).astype(jnp.float32)
+    down_part = jnp.dot(activated, w_down[0], preferred_element_type=jnp.float32)
+    down_blocks = lax.all_to_all(
+        down_part.astype(jnp.bfloat16).reshape(ctx_count, capacity, model_width), "ctx", 0, 0, tiled=True
+    )
+    summed_down = jnp.sum(down_blocks.astype(jnp.float32), axis=0)
     own_weight = lax.dynamic_index_in_dim(slot_weight, own_index, 0, keepdims=False)
     expert_out = (
         (summed_down * own_weight[:, None])

time: 352 us -> 317 us (0.901)
  waiting for transfers between devices: 198 us -> 98.1 us
  blocking collectives: 0 us -> 54.2 us
  starting transfers between devices: 63.2 us -> 72.6 us
    reduce_scatter x2 -> x0, waiting for transfers between devices: 104 us -> none  [the longest x1 77.4 us: per_device(): lax.psum_scatter(jnp.dot(activated, w_down[0], preferred_element_type=jnp...]
    all_to_all x0 -> x1, blocking collectives: none -> 54.2 us  [per_device(): lax.all_to_all(jnp.broadcast_to(outgoing[None], (ctx_count,) + outgoing.s...]
    all_to_all x0 -> x2, waiting for transfers between devices: none -> 49.4 us  [the longest x1 38.1 us: per_device(): lax.all_to_all(down_part.astype(jnp.bfloat16).reshape(ctx_count, capacity...]
    all_gather x1 -> x0, waiting for transfers between devices: 45.1 us -> none  [per_device(): row_piece = lax.all_gather(outgoing, 'ctx', axis=0, tiled=True)]
    all_to_all x0 -> x2, starting transfers between devices: none -> 9.69 us  [the longest x1 4.95 us: per_device(): lax.all_to_all(down_part.astype(jnp.bfloat16).reshape(ctx_count, capacity...]
    reduce_sum x0 -> x2, other arithmetic: none -> 4.37 us  [the longest x1 2.34 us: per_device(): summed_down = jnp.sum(down_blocks.astype(jnp.float32), axis=0)]
  transfers between devices with their start and end apart: 10 -> 9, of which waited for: 8 -> 7; matrix products, arithmetic and copies ran while one was open for 12% -> 13% of each run, Pallas kernels for 0% -> 0%
where the time goes in v2:
time: 317 us; the launch traced here: 315 us
  waiting for transfers between devices  98.1 us (31%)
  starting transfers between devices  72.6 us (23%)
  blocking collectives  54.2 us (17%)
  matrix products  39.3 us (12%)
  other arithmetic  22.7 us (7%)
  between operations  14.2 us (4%)
  local copies, waits for them, and re-layouts  13.7 us (4%)
    ppermute x6, starting transfers between devices, shift(): lax.ppermute(value.astype(jnp.bfloat16), 'ctx', pairs).astype(jnp.float32)  62.8 us
    all_to_all x1, blocking collectives, per_device(): lax.all_to_all(jnp.broadcast_to(outgoing[None], (ctx_count,) + outgoing.s...  54.2 us
    ppermute x6, waiting for transfers between devices, shift(): lax.ppermute(value.astype(jnp.bfloat16), 'ctx', pairs).astype(jnp.float32)  48 us
    all_to_all x1, waiting for transfers between devices, per_device(): lax.all_to_all(down_part.astype(jnp.bfloat16).reshape(ctx_count, capacity...  38.1 us
    dot_general x1, matrix products, per_device(): jnp.dot(stacked, lax.all_gather(out_weight, 'ctx', axis=1, tiled=True), p...  14.1 us
    all_to_all x1, waiting for transfers between devices, per_device(): lax.all_to_all(partial_term.astype(jnp.bfloat16), 'exp', 1, 0, tiled=True)  11.3 us
    dot_general x1, matrix products, per_device(): jnp.dot(activated, w_down[0], preferred_element_type=jnp.float32)  9.37 us
  transfers between devices with their start and end apart: 9, of which 7 were waited for; matrix products, arithmetic and copies ran while one was open for 13% of the time, Pallas kernels for 0%

profile of v2, /device:TPU:0, one launch (start us, length us, event | category | flops | bytes accessed | tf_op | source)
XLA Modules:
  0.0 314.8 jit_solution(10436026863582762740)
XLA Ops:
  7.9 2.4 copy.59
  16.3 9.2 %collective-permute-start.1 = (bf16[16,128,128]{2,1,0:T(8,128)(2,1)S(1)}, bf16[16,128,128]{2,1,0:T(8,128)(2,1)S(1)}, u32[]{:S(2)}, u32[]{:S(2)}) collective-permute-start(bf16[16,128,128]{2,1,0:T(8,128)(2,1)S(1)} %collective-permute-done), channel_id=1, source_target_pairs={{0,4},{4,8},{8,12},{12,16},{16,20},{20,24},{24,28},{28,32},{32,36}... | collective-permute-start | bytes 1572872 | tf_op jit(solution)/shard_map/ppermute | solution.py:14
  27.3 19.8 %collective-permute-start.2 = (bf16[16,128,128]{2,1,0:T(8,128)(2,1)S(1)}, bf16[16,128,128]{2,1,0:T(8,128)(2,1)S(1)}, u32[]{:S(2)}, u32[]{:S(2)}) collective-permute-start(bf16[16,128,128]{2,1,0:T(8,128)(2,1)S(1)} %fusion.40), channel_id=1, source_target_pairs={{0,8},{4,12},{8,16},{12,20},{16,24},{20,28},{24,32},{28,36},{32,40... | collective-permute-start | bytes 1572872 | tf_op jit(solution)/shard_map/ppermute | solution.py:14
  47.2 17.4 %collective-permute-done.2 = bf16[16,128,128]{2,1,0:T(8,128)(2,1)S(1)} collective-permute-done((bf16[16,128,128]{2,1,0:T(8,128)(2,1)S(1)}, bf16[16,128,128]{2,1,0:T(8,128)(2,1)S(1)}, u32[]{:S(2)}, u32[]{:S(2)}) %collective-permute-start.2) | collective-permute-done | bytes 524320 | tf_op jit(solution)/shard_map/ppermute | solution.py:14
  65.0 5.9 %collective-permute-start.3 = (bf16[16,128,128]{2,1,0:T(8,128)(2,1)S(1)}, bf16[16,128,128]{2,1,0:T(8,128)(2,1)S(1)}, u32[]{:S(2)}, u32[]{:S(2)}) collective-permute-start(bf16[16,128,128]{2,1,0:T(8,128)(2,1)S(1)} %fusion.87), channel_id=1, source_target_pairs={{0,16},{4,20},{8,24},{12,28},{16,32},{20,36},{24,40},{28,44},{32,4... | collective-permute-start | bytes 1572872 | tf_op jit(solution)/shard_map/ppermute | solution.py:14
  70.9 21.4 %collective-permute-done.3 = bf16[16,128,128]{2,1,0:T(8,128)(2,1)S(1)} collective-permute-done((bf16[16,128,128]{2,1,0:T(8,128)(2,1)S(1)}, bf16[16,128,128]{2,1,0:T(8,128)(2,1)S(1)}, u32[]{:S(2)}, u32[]{:S(2)}) %collective-permute-start.3) | collective-permute-done | bytes 524320 | tf_op jit(solution)/shard_map/ppermute | solution.py:14
  93.6 10.1 %collective-permute-start.4 = (bf16[16,128,128]{2,1,0:T(8,128)(2,1)}, bf16[16,128,128]{2,1,0:T(8,128)(2,1)}, u32[]{:S(2)}, u32[]{:S(2)}) collective-permute-start(bf16[16,128,128]{2,1,0:T(8,128)(2,1)} %fusion.41), channel_id=1, source_target_pairs={{0,32},{4,36},{8,40},{12,44},{16,48},{20,52},{24,56},{28,60},{32,6... | collective-permute-start | bytes 1572872 | tf_op jit(solution)/shard_map/ppermute | solution.py:14
  108.2 6.3 %collective-permute-done.4 = bf16[16,128,128]{2,1,0:T(8,128)(2,1)} collective-permute-done((bf16[16,128,128]{2,1,0:T(8,128)(2,1)}, bf16[16,128,128]{2,1,0:T(8,128)(2,1)}, u32[]{:S(2)}, u32[]{:S(2)}) %collective-permute-start.4) | collective-permute-done | bytes 524320 | tf_op jit(solution)/shard_map/ppermute | solution.py:14
  114.5 3.1 fusion.86
  117.6 16.5 %collective-permute-start.5 = (bf16[16,128,128]{2,1,0:T(8,128)(2,1)}, bf16[16,128,128]{2,1,0:T(8,128)(2,1)}, u32[]{:S(2)}, u32[]{:S(2)}) collective-permute-start(bf16[16,128,128]{2,1,0:T(8,128)(2,1)} %fusion.86), channel_id=1, source_target_pairs={{0,64},{4,68},{8,72},{12,76},{16,80},{20,84},{24,88},{28,92},{32,9... | collective-permute-start | bytes 1572872 | tf_op jit(solution)/shard_map/ppermute | solution.py:14
  138.0 3.2 %convolution_bitcast_fusion.1 = f32[128,16,128]{0,2,1:T(8,128)} fusion(bf16[128,16,128]{0,2,1:T(8,128)(2,1)} %bitcast.99, f32[128,128]{1,0:T(8,128)} %fusion.74, f32[16]{0:T(128)} %copy-done.18, pred[128,128]{1,0:T(8,128)(4,1)} %fusion.75, bf16[128,2048]{1,0:T(8,128)(2,1)} %param.17, bf16[128,2048]{1,0:T(8,128)(2,1)} %param.15), kind=kOutput, calls=%fused_computation.19 | convolution fusion | flops 135266304 | bytes 2703424 | tf_op jit(solution)/shard_map/hij,jhd->ihd/dot_general | solution.py:73
  141.2 5.1 %multiply_reduce_fusion = (f32[128,16]{0,1:T(8,128)S(1)}, f32[128,16,128]{0,2,1:T(8,128)S(1)}) fusion(f32[128,16,128]{0,2,1:T(8,128)} %convolution_bitcast_fusion.1, f32[128,16]{0,1:T(8,128)S(1)} %get-tuple-element.8, bf16[16,128,128]{2,1,0:T(8,128)(2,1)} %collective-permute-done.5, f32[16]{0:T(128)} %get-tuple-element.2, ...), kind=kOutput, calls=%fused_computation.26 | convolution fusion | flops 408156160 | bytes 5783872 | tf_op jit(solution)/shard_map/ihd,hde->ihe/dot_general | solution.py:77
  147.4 2.5 copy.56
  154.0 14.1 %fusion.6 = bf16[1,4,40,6144]{3,2,0,1:T(8,128)(2,1)} fusion(bf16[2048,6144]{0,1:T(8,128)(2,1)} %all-gather.2.cloned.1.call-done, bf16[4,8,2048]{2,1,0:T(8,128)(2,1)} %fusion.16, bf16[4,32,2048]{2,1,0:T(8,128)(2,1)} %bitcast.100), kind=kOutput, calls=%fused_computation.5 | convolution fusion | flops 4028825600 | bytes 27787264 | tf_op jit(solution)/shard_map/dot_general | solution.py:106
  168.1 4.7 %all-to-all-start = ((bf16[1,4,40,6144]{3,2,0,1:T(8,128)(2,1)}), bf16[1,4,40,6144]{3,2,0,1:T(8,128)(2,1)}, u32[]{:S(2)}, u32[]{:S(2)}) async-start(bf16[1,4,40,6144]{3,2,0,1:T(8,128)(2,1)} %fusion.6), calls=%async_computation | async-start | bytes 3932160 | tf_op jit(solution)/shard_map/all_to_all | solution.py:112
  172.9 2.4 fusion.78
  175.3 1.9 dynamic-slice_convert_fusion
  177.3 11.3 %all-to-all-done = bf16[1,4,40,6144]{3,2,0,1:T(8,128)(2,1)} async-done(((bf16[1,4,40,6144]{3,2,0,1:T(8,128)(2,1)}), bf16[1,4,40,6144]{3,2,0,1:T(8,128)(2,1)}, u32[]{:S(2)}, u32[]{:S(2)}) %all-to-all-start) | async-done | bytes 1966112 | tf_op jit(solution)/shard_map/all_to_all | solution.py:112
  188.5 2.0 convert_reduce_fusion.1
  192.9 54.2 %all_to_all.19 = bf16[32,8,6144]{2,1,0:T(8,128)(2,1)S(1)} all-to-all(bf16[32,8,6144]{2,1,0:T(8,128)(2,1)S(1)} %broadcast_in_dim.32), channel_id=1, replica_groups=mesh['ctx'=32,'exp'=4] {'ctx'}, dimensions={0} | all-to-all | bytes 6291456 | tf_op jit(solution)/shard_map/all_to_all | solution.py:125
  250.6 9.4 %fusion.2 = bf16[32,8,6144]{2,1,0:T(8,128)(2,1)} fusion(bf16[1,288,6144]{2,1,0:T(8,128)(2,1)S(1)} %copy-done, bf16[1,6144,288]{1,2,0:T(8,128)(2,1)} %param.26, bf16[32,8,6144]{2,1,0:T(8,128)(2,1)} %copy-done.3, f32[256,288]{0,1:T(8,128)} %fusion.12), kind=kOutput, calls=%fused_computation.3 | convolution fusion | flops 1813954560 | bytes 13664256 | tf_op jit(solution)/shard_map/dot_general | solution.py:131
  260.0 5.0 %all-to-all-start.2 = ((bf16[32,8,6144]{2,1,0:T(8,128)(2,1)}), bf16[32,8,6144]{2,1,0:T(8,128)(2,1)}, u32[]{:S(2)}, u32[]{:S(2)}) async-start(bf16[32,8,6144]{2,1,0:T(8,128)(2,1)} %fusion.2), calls=%async_computation.2 | async-start | bytes 6291456 | tf_op jit(solution)/shard_map/all_to_all | solution.py:132
  266.8 38.1 %all-to-all-done.2 = bf16[32,8,6144]{2,1,0:T(8,128)(2,1)} async-done(((bf16[32,8,6144]{2,1,0:T(8,128)(2,1)}), bf16[32,8,6144]{2,1,0:T(8,128)(2,1)}, u32[]{:S(2)}, u32[]{:S(2)}) %all-to-all-start.2) | async-done | bytes 3145760 | tf_op jit(solution)/shard_map/all_to_all | solution.py:132
  304.9 2.3 convert_reduce_fusion
  (82 shorter events, 32.3 us)
Async XLA Ops:
  7.2 243.4 %copy-start = (bf16[1,288,6144]{2,1,0:T(8,128)(2,1)S(1)}, bf16[1,288,6144]{2,1,0:T(8,128)(2,1)}, u32[]{:S(2)}) copy-start(bf16[1,288,6144]{2,1,0:T(8,128)(2,1)} %param.27) | copy-start | bytes 10616836
  7.2 146.8 %all-gather.2.cloned.1.call-start = ((), (), s32[]{:S(2)}) async-start(), calls=%async_computation.3 | async-start | bytes 25952256 | tf_op jit(solution)/shard_map/all_gather | solution.py:108
  11.5 80.7 %copy-start.18 = (f32[16]{0:T(128)}, f32[16]{0:T(128)S(1)}, u32[]{:S(2)}) copy-start(f32[16]{0:T(128)S(1)} %get-tuple-element.7) | copy-start | bytes 196
  11.5 82.1 %copy-start.11 = (f32[16]{0:T(128)}, f32[16]{0:T(128)S(1)}, u32[]{:S(2)}) copy-start(f32[16]{0:T(128)S(1)} %get-tuple-element.4) | copy-start | bytes 196
  11.6 82.1 %copy-start.14 = (f32[16]{0:T(128)}, f32[16]{0:T(128)S(1)}, u32[]{:S(2)}) copy-start(f32[16]{0:T(128)S(1)} %get-tuple-element.5) | copy-start | bytes 196
  11.6 103.0 %copy-start.10 = (f32[16]{0:T(128)}, f32[16]{0:T(128)S(1)}, u32[]{:S(2)}) copy-start(f32[16]{0:T(128)S(1)} %get-tuple-element.3) | copy-start | bytes 196
  13.5 2.8 collective-permute-start
  16.3 77.3 %copy-start.1 = (bf16[16,128,128]{2,1,0:T(8,128)(2,1)}, bf16[16,128,128]{2,1,0:T(8,128)(2,1)S(1)}, u32[]{:S(2)}) copy-start(bf16[16,128,128]{2,1,0:T(8,128)(2,1)S(1)} %collective-permute-done) | copy-start | bytes 1572868
  16.3 10.7 %collective-permute-start.1 = (bf16[16,128,128]{2,1,0:T(8,128)(2,1)S(1)}, bf16[16,128,128]{2,1,0:T(8,128)(2,1)S(1)}, u32[]{:S(2)}, u32[]{:S(2)}) collective-permute-start(bf16[16,128,128]{2,1,0:T(8,128)(2,1)S(1)} %collective-permute-done), channel_id=1, source_target_pairs={{0,4},{4,8},{8,12},{12,16},{16,20},{20,24},{24,28},{28,32},{32,36}... | collective-permute-start | bytes 1572872 | tf_op jit(solution)/shard_map/ppermute | solution.py:14
  27.1 66.5 %copy-start.2 = (bf16[16,128,128]{2,1,0:T(8,128)(2,1)}, bf16[16,128,128]{2,1,0:T(8,128)(2,1)S(1)}, u32[]{:S(2)}) copy-start(bf16[16,128,128]{2,1,0:T(8,128)(2,1)S(1)} %collective-permute-done.1) | copy-start | bytes 1572868
  27.1 76.6 %copy-start.16 = (s32[128,2]{0,1:T(2,128)S(1)}, s32[128,2]{0,1:T(2,128)}, u32[]{:S(2)}) copy-start(s32[128,2]{0,1:T(2,128)} %param.23) | copy-start | bytes 3076
  27.3 37.2 %collective-permute-start.2 = (bf16[16,128,128]{2,1,0:T(8,128)(2,1)S(1)}, bf16[16,128,128]{2,1,0:T(8,128)(2,1)S(1)}, u32[]{:S(2)}, u32[]{:S(2)}) collective-permute-start(bf16[16,128,128]{2,1,0:T(8,128)(2,1)S(1)} %fusion.40), channel_id=1, source_target_pairs={{0,8},{4,12},{8,16},{12,20},{16,24},{20,28},{24,32},{28,36},{32,40... | collective-permute-start | bytes 1572872 | tf_op jit(solution)/shard_map/ppermute | solution.py:14
  64.6 39.1 %copy-start.4 = (bf16[16,128,128]{2,1,0:T(8,128)(2,1)}, bf16[16,128,128]{2,1,0:T(8,128)(2,1)S(1)}, u32[]{:S(2)}) copy-start(bf16[16,128,128]{2,1,0:T(8,128)(2,1)S(1)} %collective-permute-done.2) | copy-start | bytes 1572868
  65.0 27.3 %collective-permute-start.3 = (bf16[16,128,128]{2,1,0:T(8,128)(2,1)S(1)}, bf16[16,128,128]{2,1,0:T(8,128)(2,1)S(1)}, u32[]{:S(2)}, u32[]{:S(2)}) collective-permute-start(bf16[16,128,128]{2,1,0:T(8,128)(2,1)S(1)} %fusion.87), channel_id=1, source_target_pairs={{0,16},{4,20},{8,24},{12,28},{16,32},{20,36},{24,40},{28,44},{32,4... | collective-permute-start | bytes 1572872 | tf_op jit(solution)/shard_map/ppermute | solution.py:14
  92.3 11.4 %copy-start.5 = (bf16[16,128,128]{2,1,0:T(8,128)(2,1)}, bf16[16,128,128]{2,1,0:T(8,128)(2,1)S(1)}, u32[]{:S(2)}) copy-start(bf16[16,128,128]{2,1,0:T(8,128)(2,1)S(1)} %collective-permute-done.3) | copy-start | bytes 1572868
  93.6 20.9 %collective-permute-start.4 = (bf16[16,128,128]{2,1,0:T(8,128)(2,1)}, bf16[16,128,128]{2,1,0:T(8,128)(2,1)}, u32[]{:S(2)}, u32[]{:S(2)}) collective-permute-start(bf16[16,128,128]{2,1,0:T(8,128)(2,1)} %fusion.41), channel_id=1, source_target_pairs={{0,32},{4,36},{8,40},{12,44},{16,48},{20,52},{24,56},{28,60},{32,6... | collective-permute-start | bytes 1572872 | tf_op jit(solution)/shard_map/ppermute | solution.py:14
  117.6 23.5 %collective-permute-start.5 = (bf16[16,128,128]{2,1,0:T(8,128)(2,1)}, bf16[16,128,128]{2,1,0:T(8,128)(2,1)}, u32[]{:S(2)}, u32[]{:S(2)}) collective-permute-start(bf16[16,128,128]{2,1,0:T(8,128)(2,1)} %fusion.86), channel_id=1, source_target_pairs={{0,64},{4,68},{8,72},{12,76},{16,80},{20,84},{24,88},{28,92},{32,9... | collective-permute-start | bytes 1572872 | tf_op jit(solution)/shard_map/ppermute | solution.py:14
  146.3 6.2 %copy-start.13 = (pred[128,4]{0,1:T(4,128)(4,1)S(1)}, pred[128,4]{0,1:T(4,128)(4,1)}, u32[]{:S(2)}) copy-start(pred[128,4]{0,1:T(4,128)(4,1)} %broadcast_compare_fusion) | copy-start | bytes 1540
  168.1 4.8 %copy-start.15 = (s32[32]{0:T(128)S(1)}, s32[32]{0:T(128)}, u32[]{:S(2)}) copy-start(s32[32]{0:T(128)} %eq.56) | copy-start | bytes 388
  168.1 20.4 %all-to-all-start = ((bf16[1,4,40,6144]{3,2,0,1:T(8,128)(2,1)}), bf16[1,4,40,6144]{3,2,0,1:T(8,128)(2,1)}, u32[]{:S(2)}, u32[]{:S(2)}) async-start(bf16[1,4,40,6144]{3,2,0,1:T(8,128)(2,1)} %fusion.6), calls=%async_computation | async-start | bytes 3932160 | tf_op jit(solution)/shard_map/all_to_all | solution.py:112
  192.9 55.9 %copy-start.20 = (bf16[1,6144,288]{1,2,0:T(8,128)(2,1)S(1)}, bf16[1,6144,288]{1,2,0:T(8,128)(2,1)}, u32[]{:S(2)}) copy-start(bf16[1,6144,288]{1,2,0:T(8,128)(2,1)} %param.25) | copy-start | bytes 10616836
  260.0 5.0 %copy-start.17 = (s32[128,2]{0,1:T(2,128)S(1)}, s32[128,2]{0,1:T(2,128)}, u32[]{:S(2)}) copy-start(s32[128,2]{0,1:T(2,128)} %param.23) | copy-start | bytes 3076
  260.0 5.0 %copy-start.19 = (f32[128,2]{0,1:T(2,128)S(1)}, f32[128,2]{0,1:T(2,128)}, u32[]{:S(2)}) copy-start(f32[128,2]{0,1:T(2,128)} %param.24) | copy-start | bytes 3076
  260.0 45.0 %all-to-all-start.2 = ((bf16[32,8,6144]{2,1,0:T(8,128)(2,1)}), bf16[32,8,6144]{2,1,0:T(8,128)(2,1)}, u32[]{:S(2)}, u32[]{:S(2)}) async-start(bf16[32,8,6144]{2,1,0:T(8,128)(2,1)} %fusion.2), calls=%async_computation.2 | async-start | bytes 6291456 | tf_op jit(solution)/shard_map/all_to_all | solution.py:132
  (6 other events, 12.9 us)
Sparse Core Ops, SparseCore 0:
  10.3 109.4 all-gather.1

commit v3 on v2

--- a/solution.py
+++ b/solution.py
@@ -4,14 +4,15 @@
 from jax.sharding import PartitionSpec as P
 
 HIGHEST = lax.Precision.HIGHEST
+CTX = ("yz", "core")
 
 
 def decayed_prefix(local_state, decay_rates, rows_here):
-    count = lax.axis_size("ctx")
+    count = lax.axis_size(CTX)
 
     def shift(value, step):
         pairs = [(i, i + step) for i in range(count - step)]
-        return lax.ppermute(value.astype(jnp.bfloat16), "ctx", pairs).astype(jnp.float32)
+        return lax.ppermute(value.astype(jnp.bfloat16), CTX, pairs).astype(jnp.float32)
 
     running = shift(local_state, 1)
     step = 1
@@ -103,16 +104,20 @@
         axis=1,
     )
     stacked = row_blocks.reshape(exp_count * per_block, head_count * head_size)
-    partial_rows = jnp.dot(
-        stacked,
-        lax.all_gather(out_weight, "ctx", axis=1, tiled=True),
-        preferred_element_type=jnp.float32,
+    pair_rows = lax.all_gather(stacked, "core", axis=0, tiled=True)
+    half_weight = lax.all_gather(out_weight, "yz", axis=1, tiled=True)
+    half_width = half_weight.shape[1]
+    partial_rows = jnp.dot(pair_rows, half_weight, preferred_element_type=jnp.float32)
+    partial_term = partial_rows.astype(jnp.bfloat16).reshape(2, exp_count, per_block, half_width)
+    swapped = lax.all_to_all(partial_term, "exp", 1, 1, tiled=True)
+    head_sum = jnp.sum(swapped.astype(jnp.float32), axis=1)
+    by_parity = lax.all_to_all(head_sum, "core", 0, 0, tiled=True)
+    block_width = out_weight.shape[1]
+    projected = (
+        by_parity.reshape(2, per_block, half_width // block_width, block_width)
+        .transpose(1, 2, 0, 3)
+        .reshape(per_block, model_width)
     )
-    partial_term = partial_rows.reshape(1, exp_count, per_block, model_width)
-    swapped = lax.all_to_all(
-        partial_term.astype(jnp.bfloat16), "exp", 1, 0, tiled=True
-    )
-    projected = jnp.sum(swapped.astype(jnp.float32), axis=0).reshape(per_block, model_width)
     stream_own = lax.dynamic_slice_in_dim(stream_in, own_index * own_rows, own_rows, 0)
     own_selector = lax.dynamic_slice_in_dim(selector, own_index * capacity, capacity, 0)
     stream_slots = jnp.dot(own_selector, stream_in, preferred_element_type=jnp.float32)
@@ -121,16 +126,14 @@
     residual_out = hidden_rows[:own_rows]
     slot_hidden = hidden_rows[own_rows:]
     outgoing = normalize_rows(slot_hidden, ffn_gain)
-    ctx_count = lax.axis_size("ctx")
-    row_piece = lax.all_to_all(
-        jnp.broadcast_to(outgoing[None], (ctx_count,) + outgoing.shape), "ctx", 0, 0, tiled=True
-    ).reshape(ctx_count * capacity, model_width)
+    ctx_count = lax.axis_size(CTX)
+    row_piece = lax.all_gather(outgoing, CTX, axis=0, tiled=True)
     gate_part = jnp.dot(row_piece, w_gate[0], preferred_element_type=jnp.float32)
     up_part = jnp.dot(row_piece, w_up[0], preferred_element_type=jnp.float32)
     activated = (jax.nn.silu(gate_part) * up_part).astype(jnp.bfloat16)
     down_part = jnp.dot(activated, w_down[0], preferred_element_type=jnp.float32)
     down_blocks = lax.all_to_all(
-        down_part.astype(jnp.bfloat16).reshape(ctx_count, capacity, model_width), "ctx", 0, 0, tiled=True
+        down_part.astype(jnp.bfloat16).reshape(ctx_count, capacity, model_width), CTX, 0, 0, tiled=True
     )
     summed_down = jnp.sum(down_blocks.astype(jnp.float32), axis=0)
     own_weight = lax.dynamic_index_in_dim(slot_weight, own_index, 0, keepdims=False)
@@ -143,25 +146,27 @@
 
 
 def solution(mesh):
+    ctx_size, exp_size = mesh.devices.shape
+    split = jax.sharding.Mesh(mesh.devices.reshape(ctx_size // 2, 2, exp_size), ("yz", "core", "exp"))
     return jax.shard_map(
         per_device,
-        mesh=mesh,
+        mesh=split,
         in_specs=(
-            P("ctx", None),
-            P("ctx", "exp"),
-            P("ctx", "exp"),
-            P("ctx", "exp"),
-            P("ctx", "exp"),
+            P(CTX, None),
+            P(CTX, "exp"),
+            P(CTX, "exp"),
+            P(CTX, "exp"),
+            P(CTX, "exp"),
             P("exp"),
             P("exp"),
-            P("exp", "ctx"),
+            P("exp", CTX),
             P(),
-            P("ctx", None),
-            P("ctx", None),
-            P("exp", None, "ctx"),
-            P("exp", None, "ctx"),
-            P("exp", "ctx", None),
+            P(CTX, None),
+            P(CTX, None),
+            P("exp", None, CTX),
+            P("exp", None, CTX),
+            P("exp", CTX, None),
         ),
-        out_specs=(P(("ctx", "exp"), None), P("ctx", "exp", None, None)),
+        out_specs=(P((CTX[0], CTX[1], "exp"), None), P(CTX, "exp", None, None)),
         check_vma=False,
     )

time: 317 us -> 397 us (1.25)
  waiting for transfers between devices: 98.1 us -> 241 us
  blocking collectives: 54.2 us -> 5.31 us
  starting transfers between devices: 72.6 us -> 48.7 us
  local copies, waits for them, and re-layouts: 13.7 us -> 22 us
  other arithmetic: 22.7 us -> 26.8 us
    all_gather x1 -> x3, waiting for transfers between devices: 0.01 us -> 154 us  [the longest x1 93.7 us: per_device(): half_weight = lax.all_gather(out_weight, 'yz', axis=1, tiled=True)]
    all_to_all x1, blocking collectives: 54.2 us -> 5.31 us  [per_device(): by_parity = lax.all_to_all(head_sum, 'core', 0, 0, tiled=True)]
    ppermute x6, starting transfers between devices: 62.8 us -> 38.5 us  [shift(): lax.ppermute(value.astype(jnp.bfloat16), CTX, pairs).astype(jnp.float32)]
    ppermute x6, waiting for transfers between devices: 48 us -> 27.8 us  [shift(): lax.ppermute(value.astype(jnp.bfloat16), CTX, pairs).astype(jnp.float32)]
    all_to_all x1, waiting for transfers between devices: 11.3 us -> 20.8 us  [per_device(): swapped = lax.all_to_all(partial_term, 'exp', 1, 1, tiled=True)]
    reshape x0 -> x3, local copies, waits for them, and re-layouts: none -> 7.9 us  [the longest x1 3.6 us: per_device(): projected = by_parity.reshape(2, per_block, half_width // block_width, bl...]
    dot_general x1, matrix products: 14.1 us -> 9.24 us  [per_device(): jnp.dot(pair_rows, half_weight, preferred_element_type=jnp.float32)]
  transfers between devices with their start and end apart: 9 -> 11, of which waited for: 7 -> 10; matrix products, arithmetic and copies ran while one was open for 13% -> 5% of each run, Pallas kernels for 0% -> 0%
where the time goes in v3:
time: 397 us; the launch traced here: 394 us
  waiting for transfers between devices  241 us (61%)
  starting transfers between devices  48.7 us (12%)
  matrix products  36.7 us (9%)
  other arithmetic  26.8 us (7%)
  local copies, waits for them, and re-layouts  22 us (6%)
  between operations  13.9 us (4%)
  blocking collectives  5.31 us (1%)
    all_gather x1, waiting for transfers between devices, per_device(): half_weight = lax.all_gather(out_weight, 'yz', axis=1, tiled=True)  93.7 us
    all_gather x1, waiting for transfers between devices, per_device(): row_piece = lax.all_gather(outgoing, CTX, axis=0, tiled=True)  43.1 us
    ppermute x6, starting transfers between devices, shift(): lax.ppermute(value.astype(jnp.bfloat16), CTX, pairs).astype(jnp.float32)  38.5 us
    all_to_all x1, waiting for transfers between devices, per_device(): lax.all_to_all(down_part.astype(jnp.bfloat16).reshape(ctx_count, capacity...  38 us
    ppermute x6, waiting for transfers between devices, shift(): lax.ppermute(value.astype(jnp.bfloat16), CTX, pairs).astype(jnp.float32)  27.8 us
    all_to_all x1, waiting for transfers between devices, per_device(): swapped = lax.all_to_all(partial_term, 'exp', 1, 1, tiled=True)  20.8 us
    all_gather x1, waiting for transfers between devices, per_device(): pair_rows = lax.all_gather(stacked, 'core', axis=0, tiled=True)  16.8 us
    dot_general x1, matrix products, per_device(): jnp.dot(activated, w_down[0], preferred_element_type=jnp.float32)  9.37 us
  transfers between devices with their start and end apart: 11, of which 10 were waited for; matrix products, arithmetic and copies ran while one was open for 5% of the time, Pallas kernels for 0%

profile of v3, /device:TPU:0, one launch (start us, length us, event | category | flops | bytes accessed | tf_op | source)
XLA Modules:
  0.0 394.3 jit_solution(3186503120921249758)
XLA Ops:
  16.8 9.2 %collective-permute-start.1 = (bf16[16,128,128]{2,1,0:T(8,128)(2,1)S(1)}, bf16[16,128,128]{2,1,0:T(8,128)(2,1)S(1)}, u32[]{:S(2)}, u32[]{:S(2)}) collective-permute-start(bf16[16,128,128]{2,1,0:T(8,128)(2,1)S(1)} %collective-permute-done), channel_id=1, source_target_pairs={{0,4},{4,8},{8,12},{12,16},{16,20},{20,24},{24,28},{28,32},{32,36}... | collective-permute-start | bytes 1572872 | tf_op jit(solution)/shard_map/ppermute | solution.py:15
  27.8 11.4 %collective-permute-start.2 = (bf16[16,128,128]{2,1,0:T(8,128)(2,1)S(1)}, bf16[16,128,128]{2,1,0:T(8,128)(2,1)S(1)}, u32[]{:S(2)}, u32[]{:S(2)}) collective-permute-start(bf16[16,128,128]{2,1,0:T(8,128)(2,1)S(1)} %fusion.26), channel_id=1, source_target_pairs={{0,8},{4,12},{8,16},{12,20},{16,24},{20,28},{24,32},{28,36},{32,40... | collective-permute-start | bytes 1572872 | tf_op jit(solution)/shard_map/ppermute | solution.py:15
  39.2 10.8 %collective-permute-done.2 = bf16[16,128,128]{2,1,0:T(8,128)(2,1)S(1)} collective-permute-done((bf16[16,128,128]{2,1,0:T(8,128)(2,1)S(1)}, bf16[16,128,128]{2,1,0:T(8,128)(2,1)S(1)}, u32[]{:S(2)}, u32[]{:S(2)}) %collective-permute-start.2) | collective-permute-done | bytes 524320 | tf_op jit(solution)/shard_map/ppermute | solution.py:15
  50.5 6.1 %collective-permute-start.3 = (bf16[16,128,128]{2,1,0:T(8,128)(2,1)S(1)}, bf16[16,128,128]{2,1,0:T(8,128)(2,1)S(1)}, u32[]{:S(2)}, u32[]{:S(2)}) collective-permute-start(bf16[16,128,128]{2,1,0:T(8,128)(2,1)S(1)} %fusion.69), channel_id=1, source_target_pairs={{0,16},{4,20},{8,24},{12,28},{16,32},{20,36},{24,40},{28,44},{32,4... | collective-permute-start | bytes 1572872 | tf_op jit(solution)/shard_map/ppermute | solution.py:15
  56.6 10.2 %collective-permute-done.3 = bf16[16,128,128]{2,1,0:T(8,128)(2,1)S(1)} collective-permute-done((bf16[16,128,128]{2,1,0:T(8,128)(2,1)S(1)}, bf16[16,128,128]{2,1,0:T(8,128)(2,1)S(1)}, u32[]{:S(2)}, u32[]{:S(2)}) %collective-permute-start.3) | collective-permute-done | bytes 524320 | tf_op jit(solution)/shard_map/ppermute | solution.py:15
  68.1 4.9 %collective-permute-start.4 = (bf16[16,128,128]{2,1,0:T(8,128)(2,1)}, bf16[16,128,128]{2,1,0:T(8,128)(2,1)}, u32[]{:S(2)}, u32[]{:S(2)}) collective-permute-start(bf16[16,128,128]{2,1,0:T(8,128)(2,1)} %fusion.27), channel_id=1, source_target_pairs={{0,32},{4,36},{8,40},{12,44},{16,48},{20,52},{24,56},{28,60},{32,6... | collective-permute-start | bytes 1572872 | tf_op jit(solution)/shard_map/ppermute | solution.py:15
  77.5 3.7 collective-permute-done.4
  81.2 3.1 fusion.68
  84.4 5.6 %collective-permute-start.5 = (bf16[16,128,128]{2,1,0:T(8,128)(2,1)}, bf16[16,128,128]{2,1,0:T(8,128)(2,1)}, u32[]{:S(2)}, u32[]{:S(2)}) collective-permute-start(bf16[16,128,128]{2,1,0:T(8,128)(2,1)} %fusion.68), channel_id=1, source_target_pairs={{0,64},{4,68},{8,72},{12,76},{16,80},{20,84},{24,88},{28,92},{32,9... | collective-permute-start | bytes 1572872 | tf_op jit(solution)/shard_map/ppermute | solution.py:15
  93.9 3.1 convolution_bitcast_fusion.1
  97.0 5.1 %multiply_reduce_fusion = (f32[128,16]{0,1:T(8,128)S(1)}, f32[128,16,128]{0,2,1:T(8,128)S(1)}) fusion(f32[128,16,128]{0,2,1:T(8,128)} %convolution_bitcast_fusion.1, f32[128,16]{0,1:T(8,128)S(1)} %get-tuple-element.8, bf16[16,128,128]{2,1,0:T(8,128)(2,1)} %collective-permute-done.5, f32[16]{0:T(128)} %get-tuple-element.2, ...), kind=kOutput, calls=%fused_computation.21 | convolution fusion | flops 408156160 | bytes 5783872 | tf_op jit(solution)/shard_map/ihd,hde->ihe/dot_general | solution.py:78
  110.0 16.8 %all-gather.4.cloned.1.call-done = bf16[320,2048]{1,0:T(8,128)(2,1)} async-done(((bf16[160,2048]{1,0:T(8,128)(2,1)}), bf16[320,2048]{1,0:T(8,128)(2,1)}) %all-gather.4.cloned.1.call-update) | async-done | bytes 1310736 | tf_op jit(solution)/shard_map/all_gather | solution.py:107
  126.8 93.7 %all-gather.6.cloned.1.call-done = bf16[2048,3072]{0,1:T(8,128)(2,1)} async-done(((bf16[2048,192]{0,1:T(8,128)(2,1)}), bf16[2048,3072]{0,1:T(8,128)(2,1)}) %all-gather.6.cloned.1.call-update) | async-done | bytes 12582928 | tf_op jit(solution)/shard_map/all_gather | solution.py:108
  220.5 9.2 %convolution_convert_fusion.1 = bf16[320,3072]{1,0:T(8,128)(2,1)S(1)} fusion(bf16[320,2048]{1,0:T(8,128)(2,1)} %all-gather.4.cloned.1.call-done, bf16[2048,3072]{0,1:T(8,128)(2,1)} %all-gather.6.cloned.1.call-done), kind=kOutput, calls=%fused_computation.3 | convolution fusion | flops 4027514880 | bytes 15859712 | tf_op jit(solution)/shard_map/dot_general | solution.py:110
  231.2 4.4 %all-to-all-start = ((bf16[2,4,40,3072]{3,2,0,1:T(8,128)(2,1)}), bf16[2,4,40,3072]{3,2,0,1:T(8,128)(2,1)}, u32[]{:S(2)}, u32[]{:S(2)}) async-start(bf16[2,4,40,3072]{3,2,0,1:T(8,128)(2,1)} %copy.71), calls=%async_computation | async-start | bytes 3932160 | tf_op jit(solution)/shard_map/all_to_all | solution.py:112
  240.1 20.8 %all-to-all-done = bf16[2,4,40,3072]{3,2,0,1:T(8,128)(2,1)} async-done(((bf16[2,4,40,3072]{3,2,0,1:T(8,128)(2,1)}), bf16[2,4,40,3072]{3,2,0,1:T(8,128)(2,1)}, u32[]{:S(2)}, u32[]{:S(2)}) %all-to-all-start) | async-done | bytes 1966112 | tf_op jit(solution)/shard_map/all_to_all | solution.py:112
  262.8 5.3 %all_to_all.15 = f32[2,40,3072]{2,1,0:T(8,128)} all-to-all(f32[2,40,3072]{2,1,0:T(8,128)S(1)} %convert_reduce_fusion.1), channel_id=1, replica_groups=mesh['yz'=16,'core'=2,'exp'=4] {'core'}, dimensions={0} | all-to-all | bytes 1966080 | tf_op jit(solution)/shard_map/all_to_all | solution.py:114
  271.0 3.5 copy.72
  274.5 3.6 reshape.211
  282.0 43.1 %all-gather.8.cloned.1.call-done = bf16[256,6144]{1,0:T(8,128)(2,1)} async-done(((bf16[8,6144]{1,0:T(8,128)(2,1)}), bf16[256,6144]{1,0:T(8,128)(2,1)}) %all-gather.8.cloned.1.call-update) | async-done | bytes 3145744 | tf_op jit(solution)/shard_map/all_gather | solution.py:130
  325.2 4.8 %fusion.4 = f32[256,288]{0,1:T(8,128)} fusion(bf16[256,6144]{1,0:T(8,128)(2,1)} %all-gather.8.cloned.1.call-done, bf16[1,6144,288]{1,2,0:T(8,128)(2,1)} %param.25), kind=kOutput, calls=%fused_computation.8 | convolution fusion | flops 905969664 | bytes 6979584 | tf_op jit(solution)/shard_map/dot_general | solution.py:131
  329.9 9.4 %fusion = bf16[32,8,6144]{2,1,0:T(8,128)(2,1)} fusion(bf16[1,288,6144]{2,1,0:T(8,128)(2,1)S(1)} %copy-done, bf16[256,6144]{1,0:T(8,128)(2,1)} %all-gather.8.cloned.1.call-done, bf16[1,6144,288]{1,2,0:T(8,128)(2,1)} %param.26, f32[256,288]{0,1:T(8,128)} %fusion.4), kind=kOutput, calls=%fused_computation.1 | convolution fusion | flops 1813954560 | bytes 13664256 | tf_op jit(solution)/shard_map/dot_general | solution.py:134
  339.3 5.5 %all-to-all-start.2 = ((bf16[32,8,6144]{2,1,0:T(8,128)(2,1)}), bf16[32,8,6144]{2,1,0:T(8,128)(2,1)}, u32[]{:S(2)}, u32[]{:S(2)}) async-start(bf16[32,8,6144]{2,1,0:T(8,128)(2,1)} %fusion), calls=%async_computation.2 | async-start | bytes 6291456 | tf_op jit(solution)/shard_map/all_to_all | solution.py:135
  346.7 38.0 %all-to-all-done.2 = bf16[32,8,6144]{2,1,0:T(8,128)(2,1)} async-done(((bf16[32,8,6144]{2,1,0:T(8,128)(2,1)}), bf16[32,8,6144]{2,1,0:T(8,128)(2,1)}, u32[]{:S(2)}, u32[]{:S(2)}) %all-to-all-start.2) | async-done | bytes 3145760 | tf_op jit(solution)/shard_map/all_to_all | solution.py:135
  (80 shorter events, 49.0 us)
Async XLA Ops:
  7.2 322.8 %copy-start = (bf16[1,288,6144]{2,1,0:T(8,128)(2,1)S(1)}, bf16[1,288,6144]{2,1,0:T(8,128)(2,1)}, u32[]{:S(2)}) copy-start(bf16[1,288,6144]{2,1,0:T(8,128)(2,1)} %param.27) | copy-start | bytes 10616836
  7.2 119.6 %all-gather.4.cloned.1.call-start = ((), (), s32[]{:S(2)}) async-start(), calls=%async_computation.3 | async-start | bytes 1966080 | tf_op jit(solution)/shard_map/all_gather | solution.py:107
  9.3 57.5 %copy-start.7 = (f32[16]{0:T(128)}, f32[16]{0:T(128)S(1)}, u32[]{:S(2)}) copy-start(f32[16]{0:T(128)S(1)} %get-tuple-element.4) | copy-start | bytes 196
  9.3 72.0 %copy-start.6 = (f32[16]{0:T(128)}, f32[16]{0:T(128)S(1)}, u32[]{:S(2)}) copy-start(f32[16]{0:T(128)S(1)} %get-tuple-element.3) | copy-start | bytes 196
  11.3 55.5 %copy-start.10 = (f32[16]{0:T(128)S(1)}, f32[16]{0:T(128)}, u32[]{:S(2)}) copy-start(f32[16]{0:T(128)} %get-tuple-element.5) | copy-start | bytes 196
  14.0 2.8 collective-permute-start
  16.8 51.3 %copy-start.1 = (bf16[16,128,128]{2,1,0:T(8,128)(2,1)}, bf16[16,128,128]{2,1,0:T(8,128)(2,1)S(1)}, u32[]{:S(2)}) copy-start(bf16[16,128,128]{2,1,0:T(8,128)(2,1)S(1)} %collective-permute-done) | copy-start | bytes 1572868
  16.8 10.7 %collective-permute-start.1 = (bf16[16,128,128]{2,1,0:T(8,128)(2,1)S(1)}, bf16[16,128,128]{2,1,0:T(8,128)(2,1)S(1)}, u32[]{:S(2)}, u32[]{:S(2)}) collective-permute-start(bf16[16,128,128]{2,1,0:T(8,128)(2,1)S(1)} %collective-permute-done), channel_id=1, source_target_pairs={{0,4},{4,8},{8,12},{12,16},{16,20},{20,24},{24,28},{28,32},{32,36}... | collective-permute-start | bytes 1572872 | tf_op jit(solution)/shard_map/ppermute | solution.py:15
  27.5 40.6 %copy-start.2 = (bf16[16,128,128]{2,1,0:T(8,128)(2,1)}, bf16[16,128,128]{2,1,0:T(8,128)(2,1)S(1)}, u32[]{:S(2)}) copy-start(bf16[16,128,128]{2,1,0:T(8,128)(2,1)S(1)} %collective-permute-done.1) | copy-start | bytes 1572868
  27.5 45.5 %copy-start.12 = (s32[128,2]{0,1:T(2,128)S(1)}, s32[128,2]{0,1:T(2,128)}, u32[]{:S(2)}) copy-start(s32[128,2]{0,1:T(2,128)} %param.23) | copy-start | bytes 3076
  27.8 22.2 %collective-permute-start.2 = (bf16[16,128,128]{2,1,0:T(8,128)(2,1)S(1)}, bf16[16,128,128]{2,1,0:T(8,128)(2,1)S(1)}, u32[]{:S(2)}, u32[]{:S(2)}) collective-permute-start(bf16[16,128,128]{2,1,0:T(8,128)(2,1)S(1)} %fusion.26), channel_id=1, source_target_pairs={{0,8},{4,12},{8,16},{12,20},{16,24},{20,28},{24,32},{28,36},{32,40... | collective-permute-start | bytes 1572872 | tf_op jit(solution)/shard_map/ppermute | solution.py:15
  50.0 23.0 %copy-start.3 = (bf16[16,128,128]{2,1,0:T(8,128)(2,1)}, bf16[16,128,128]{2,1,0:T(8,128)(2,1)S(1)}, u32[]{:S(2)}) copy-start(bf16[16,128,128]{2,1,0:T(8,128)(2,1)S(1)} %collective-permute-done.2) | copy-start | bytes 1572868
  50.5 16.3 %collective-permute-start.3 = (bf16[16,128,128]{2,1,0:T(8,128)(2,1)S(1)}, bf16[16,128,128]{2,1,0:T(8,128)(2,1)S(1)}, u32[]{:S(2)}, u32[]{:S(2)}) collective-permute-start(bf16[16,128,128]{2,1,0:T(8,128)(2,1)S(1)} %fusion.69), channel_id=1, source_target_pairs={{0,16},{4,20},{8,24},{12,28},{16,32},{20,36},{24,40},{28,44},{32,4... | collective-permute-start | bytes 1572872 | tf_op jit(solution)/shard_map/ppermute | solution.py:15
  66.8 6.2 %copy-start.4 = (bf16[16,128,128]{2,1,0:T(8,128)(2,1)}, bf16[16,128,128]{2,1,0:T(8,128)(2,1)S(1)}, u32[]{:S(2)}) copy-start(bf16[16,128,128]{2,1,0:T(8,128)(2,1)S(1)} %collective-permute-done.3) | copy-start | bytes 1572868
  68.1 13.1 %collective-permute-start.4 = (bf16[16,128,128]{2,1,0:T(8,128)(2,1)}, bf16[16,128,128]{2,1,0:T(8,128)(2,1)}, u32[]{:S(2)}, u32[]{:S(2)}) collective-permute-start(bf16[16,128,128]{2,1,0:T(8,128)(2,1)} %fusion.27), channel_id=1, source_target_pairs={{0,32},{4,36},{8,40},{12,44},{16,48},{20,52},{24,56},{28,60},{32,6... | collective-permute-start | bytes 1572872 | tf_op jit(solution)/shard_map/ppermute | solution.py:15
  84.4 12.6 %collective-permute-start.5 = (bf16[16,128,128]{2,1,0:T(8,128)(2,1)}, bf16[16,128,128]{2,1,0:T(8,128)(2,1)}, u32[]{:S(2)}, u32[]{:S(2)}) collective-permute-start(bf16[16,128,128]{2,1,0:T(8,128)(2,1)} %fusion.68), channel_id=1, source_target_pairs={{0,64},{4,68},{8,72},{12,76},{16,80},{20,84},{24,88},{28,92},{32,9... | collective-permute-start | bytes 1572872 | tf_op jit(solution)/shard_map/ppermute | solution.py:15
  102.1 5.3 %copy-start.9 = (pred[128,4]{0,1:T(4,128)(4,1)S(1)}, pred[128,4]{0,1:T(4,128)(4,1)}, u32[]{:S(2)}) copy-start(pred[128,4]{0,1:T(4,128)(4,1)} %broadcast_compare_fusion) | copy-start | bytes 1540
  109.2 111.3 %all-gather.6.cloned.1.call-start = ((), (), s32[]{:S(2)}) async-start(), calls=%async_computation.4 | async-start | bytes 13369344 | tf_op jit(solution)/shard_map/all_gather | solution.py:108
  229.7 5.9 %copy-start.11 = (s32[32]{0:T(128)S(1)}, s32[32]{0:T(128)}, u32[]{:S(2)}) copy-start(s32[32]{0:T(128)} %eq.56) | copy-start | bytes 388
  231.2 29.7 %all-to-all-start = ((bf16[2,4,40,3072]{3,2,0,1:T(8,128)(2,1)}), bf16[2,4,40,3072]{3,2,0,1:T(8,128)(2,1)}, u32[]{:S(2)}, u32[]{:S(2)}) async-start(bf16[2,4,40,3072]{3,2,0,1:T(8,128)(2,1)} %copy.71), calls=%async_computation | async-start | bytes 3932160 | tf_op jit(solution)/shard_map/all_to_all | solution.py:112
  235.6 89.6 %all-gather.8.cloned.1.call-start = ((), (), s32[]{:S(2)}) async-start(), calls=%async_computation.5 | async-start | bytes 3244032 | tf_op jit(solution)/shard_map/all_gather | solution.py:130
  339.3 5.5 %copy-start.13 = (s32[128,2]{0,1:T(2,128)S(1)}, s32[128,2]{0,1:T(2,128)}, u32[]{:S(2)}) copy-start(s32[128,2]{0,1:T(2,128)} %param.23) | copy-start | bytes 3076
  339.3 5.5 %copy-start.14 = (f32[128,2]{0,1:T(2,128)S(1)}, f32[128,2]{0,1:T(2,128)}, u32[]{:S(2)}) copy-start(f32[128,2]{0,1:T(2,128)} %param.24) | copy-start | bytes 3076
  339.3 45.4 %all-to-all-start.2 = ((bf16[32,8,6144]{2,1,0:T(8,128)(2,1)}), bf16[32,8,6144]{2,1,0:T(8,128)(2,1)}, u32[]{:S(2)}, u32[]{:S(2)}) async-start(bf16[32,8,6144]{2,1,0:T(8,128)(2,1)} %fusion), calls=%async_computation.2 | async-start | bytes 6291456 | tf_op jit(solution)/shard_map/all_to_all | solution.py:135
  (2 other events, 4.5 us)
Sparse Core Ops, SparseCore 0:
  109.3 17.3 all-gather.3
  128.9 91.5 all-gather.5
  282.1 42.9 all-gather.7

commit v4 on v3

--- a/solution.py
+++ b/solution.py
@@ -21,6 +21,15 @@
         running = running + factor[:, None, None] * shift(running, step)
         step *= 2
     return running
+
+
+def partner(value):
+    return lax.ppermute(value, "core", [(0, 1), (1, 0)])
+
+
+def by_core(mine, theirs):
+    first = lax.axis_index("core") == 0
+    return jnp.where(first, mine, theirs), jnp.where(first, theirs, mine)
 
 
 def normalize_rows(row_block, ffn_gain):
@@ -104,14 +113,17 @@
         axis=1,
     )
     stacked = row_blocks.reshape(exp_count * per_block, head_count * head_size)
-    pair_rows = lax.all_gather(stacked, "core", axis=0, tiled=True)
+    pair_rows = jnp.concatenate(by_core(stacked, partner(stacked)), axis=0)
     half_weight = lax.all_gather(out_weight, "yz", axis=1, tiled=True)
     half_width = half_weight.shape[1]
     partial_rows = jnp.dot(pair_rows, half_weight, preferred_element_type=jnp.float32)
     partial_term = partial_rows.astype(jnp.bfloat16).reshape(2, exp_count, per_block, half_width)
     swapped = lax.all_to_all(partial_term, "exp", 1, 1, tiled=True)
     head_sum = jnp.sum(swapped.astype(jnp.float32), axis=1)
-    by_parity = lax.all_to_all(head_sum, "core", 0, 0, tiled=True)
+    core_here = lax.axis_index("core")
+    kept = lax.dynamic_index_in_dim(head_sum, core_here, 0, keepdims=False)
+    sent = lax.dynamic_index_in_dim(head_sum, 1 - core_here, 0, keepdims=False)
+    by_parity = jnp.stack(by_core(kept, partner(sent)), axis=0)
     block_width = out_weight.shape[1]
     projected = (
         by_parity.reshape(2, per_block, half_width // block_width, block_width)
@@ -127,14 +139,17 @@
     slot_hidden = hidden_rows[own_rows:]
     outgoing = normalize_rows(slot_hidden, ffn_gain)
     ctx_count = lax.axis_size(CTX)
-    row_piece = lax.all_gather(outgoing, CTX, axis=0, tiled=True)
+    chip_rows = jnp.concatenate(by_core(outgoing, partner(outgoing)), axis=0)
+    row_piece = lax.all_gather(chip_rows, "yz", axis=0, tiled=True)
     gate_part = jnp.dot(row_piece, w_gate[0], preferred_element_type=jnp.float32)
     up_part = jnp.dot(row_piece, w_up[0], preferred_element_type=jnp.float32)
     activated = (jax.nn.silu(gate_part) * up_part).astype(jnp.bfloat16)
     down_part = jnp.dot(activated, w_down[0], preferred_element_type=jnp.float32)
-    down_blocks = lax.all_to_all(
-        down_part.astype(jnp.bfloat16).reshape(ctx_count, capacity, model_width), CTX, 0, 0, tiled=True
-    )
+    down_rows = down_part.astype(jnp.bfloat16).reshape(ctx_count // 2, 2, capacity, model_width)
+    down_kept = lax.dynamic_index_in_dim(down_rows, core_here, 1, keepdims=False)
+    down_sent = lax.dynamic_index_in_dim(down_rows, 1 - core_here, 1, keepdims=False)
+    pair_sum = down_kept.astype(jnp.float32) + partner(down_sent).astype(jnp.float32)
+    down_blocks = lax.all_to_all(pair_sum.astype(jnp.bfloat16), "yz", 0, 0, tiled=True)
     summed_down = jnp.sum(down_blocks.astype(jnp.float32), axis=0)
     own_weight = lax.dynamic_index_in_dim(slot_weight, own_index, 0, keepdims=False)
     expert_out = (

time: 397 us -> 333 us (0.84)
  waiting for transfers between devices: 241 us -> 150 us
  starting transfers between devices: 48.7 us -> 73.1 us
  other arithmetic: 26.8 us -> 34.5 us
  blocking collectives: 5.31 us -> 0 us
    all_gather x1, waiting for transfers between devices: 93.7 us -> 0.01 us  [per_device(): half_weight = lax.all_gather(out_weight, 'yz', axis=1, tiled=True)]
    ppermute x6, starting transfers between devices: 38.5 us -> 63.1 us  [shift(): lax.ppermute(value.astype(jnp.bfloat16), CTX, pairs).astype(jnp.float32)]
    ppermute x6, waiting for transfers between devices: 27.8 us -> 47.8 us  [shift(): lax.ppermute(value.astype(jnp.bfloat16), CTX, pairs).astype(jnp.float32)]
    all_to_all x1, waiting for transfers between devices: 38 us -> 22.7 us  [per_device(): lax.all_to_all(pair_sum.astype(jnp.bfloat16), 'yz', 0, 0, tiled=True)]
    all_gather x2 -> x1, waiting for transfers between devices: 59.9 us -> 49.1 us  [per_device(): row_piece = lax.all_gather(chip_rows, 'yz', axis=0, tiled=True)]
    ppermute x0 -> x4, waiting for transfers between devices: none -> 6.78 us  [partner(): return lax.ppermute(value, 'core', [(0, 1), (1, 0)])]
    another operation x0 -> x2, local copies, waits for them, and re-layouts: none -> 6.01 us  [per_device(): by_parity = jnp.stack(by_core(kept, partner(sent)), axis=0)]
    all_to_all x1 -> x0, blocking collectives: 5.31 us -> none  [per_device(): by_parity = lax.all_to_all(head_sum, 'core', 0, 0, tiled=True)]
  transfers between devices with their start and end apart: 11 -> 14, of which waited for: 10 -> 11; matrix products, arithmetic and copies ran while one was open for 5% -> 13% of each run, Pallas kernels for 0% -> 0%
where the time goes in v4:
time: 333 us; the launch traced here: 332 us
  waiting for transfers between devices  150 us (45%)
  starting transfers between devices  73.1 us (22%)
  matrix products  36.8 us (11%)
  other arithmetic  34.5 us (10%)
  local copies, waits for them, and re-layouts  23.1 us (7%)
  between operations  14.3 us (4%)
    ppermute x6, starting transfers between devices, shift(): lax.ppermute(value.astype(jnp.bfloat16), CTX, pairs).astype(jnp.float32)  63.1 us
    all_gather x1, waiting for transfers between devices, per_device(): row_piece = lax.all_gather(chip_rows, 'yz', axis=0, tiled=True)  49.1 us
    ppermute x6, waiting for transfers between devices, shift(): lax.ppermute(value.astype(jnp.bfloat16), CTX, pairs).astype(jnp.float32)  47.8 us
    all_to_all x1, waiting for transfers between devices, per_device(): swapped = lax.all_to_all(partial_term, 'exp', 1, 1, tiled=True)  23 us
    all_to_all x1, waiting for transfers between devices, per_device(): lax.all_to_all(pair_sum.astype(jnp.bfloat16), 'yz', 0, 0, tiled=True)  22.7 us
    dot_general x1, matrix products, per_device(): jnp.dot(activated, w_down[0], preferred_element_type=jnp.float32)  9.43 us
    dot_general x1, matrix products, per_device(): jnp.dot(pair_rows, half_weight, preferred_element_type=jnp.float32)  9.25 us
    ppermute x4, waiting for transfers between devices, partner(): return lax.ppermute(value, 'core', [(0, 1), (1, 0)])  6.78 us
  transfers between devices with their start and end apart: 14, of which 11 were waited for; matrix products, arithmetic and copies ran while one was open for 13% of the time, Pallas kernels for 0%

profile of v4, /device:TPU:0, one launch (start us, length us, event | category | flops | bytes accessed | tf_op | source)
XLA Modules:
  0.0 331.9 jit_solution(12308046563394121018)
XLA Ops:
  16.3 9.2 %collective-permute-start.1 = (bf16[16,128,128]{2,1,0:T(8,128)(2,1)S(1)}, bf16[16,128,128]{2,1,0:T(8,128)(2,1)S(1)}, u32[]{:S(2)}, u32[]{:S(2)}) collective-permute-start(bf16[16,128,128]{2,1,0:T(8,128)(2,1)S(1)} %collective-permute-done), channel_id=1, source_target_pairs={{0,4},{4,8},{8,12},{12,16},{16,20},{20,24},{24,28},{28,32},{32,36}... | collective-permute-start | bytes 1572872 | tf_op jit(solution)/shard_map/ppermute | solution.py:15
  27.3 19.8 %collective-permute-start.2 = (bf16[16,128,128]{2,1,0:T(8,128)(2,1)S(1)}, bf16[16,128,128]{2,1,0:T(8,128)(2,1)S(1)}, u32[]{:S(2)}, u32[]{:S(2)}) collective-permute-start(bf16[16,128,128]{2,1,0:T(8,128)(2,1)S(1)} %fusion.29), channel_id=1, source_target_pairs={{0,8},{4,12},{8,16},{12,20},{16,24},{20,28},{24,32},{28,36},{32,40... | collective-permute-start | bytes 1572872 | tf_op jit(solution)/shard_map/ppermute | solution.py:15
  47.2 17.4 %collective-permute-done.2 = bf16[16,128,128]{2,1,0:T(8,128)(2,1)S(1)} collective-permute-done((bf16[16,128,128]{2,1,0:T(8,128)(2,1)S(1)}, bf16[16,128,128]{2,1,0:T(8,128)(2,1)S(1)}, u32[]{:S(2)}, u32[]{:S(2)}) %collective-permute-start.2) | collective-permute-done | bytes 524320 | tf_op jit(solution)/shard_map/ppermute | solution.py:15
  65.0 5.9 %collective-permute-start.3 = (bf16[16,128,128]{2,1,0:T(8,128)(2,1)S(1)}, bf16[16,128,128]{2,1,0:T(8,128)(2,1)S(1)}, u32[]{:S(2)}, u32[]{:S(2)}) collective-permute-start(bf16[16,128,128]{2,1,0:T(8,128)(2,1)S(1)} %fusion.73), channel_id=1, source_target_pairs={{0,16},{4,20},{8,24},{12,28},{16,32},{20,36},{24,40},{28,44},{32,4... | collective-permute-start | bytes 1572872 | tf_op jit(solution)/shard_map/ppermute | solution.py:15
  70.9 21.4 %collective-permute-done.3 = bf16[16,128,128]{2,1,0:T(8,128)(2,1)S(1)} collective-permute-done((bf16[16,128,128]{2,1,0:T(8,128)(2,1)S(1)}, bf16[16,128,128]{2,1,0:T(8,128)(2,1)S(1)}, u32[]{:S(2)}, u32[]{:S(2)}) %collective-permute-start.3) | collective-permute-done | bytes 524320 | tf_op jit(solution)/shard_map/ppermute | solution.py:15
  93.6 10.3 %collective-permute-start.4 = (bf16[16,128,128]{2,1,0:T(8,128)(2,1)}, bf16[16,128,128]{2,1,0:T(8,128)(2,1)}, u32[]{:S(2)}, u32[]{:S(2)}) collective-permute-start(bf16[16,128,128]{2,1,0:T(8,128)(2,1)} %fusion.32), channel_id=1, source_target_pairs={{0,32},{4,36},{8,40},{12,44},{16,48},{20,52},{24,56},{28,60},{32,6... | collective-permute-start | bytes 1572872 | tf_op jit(solution)/shard_map/ppermute | solution.py:15
  108.4 6.1 %collective-permute-done.4 = bf16[16,128,128]{2,1,0:T(8,128)(2,1)} collective-permute-done((bf16[16,128,128]{2,1,0:T(8,128)(2,1)}, bf16[16,128,128]{2,1,0:T(8,128)(2,1)}, u32[]{:S(2)}, u32[]{:S(2)}) %collective-permute-start.4) | collective-permute-done | bytes 524320 | tf_op jit(solution)/shard_map/ppermute | solution.py:15
  114.4 3.1 fusion.72
  117.5 16.6 %collective-permute-start.5 = (bf16[16,128,128]{2,1,0:T(8,128)(2,1)}, bf16[16,128,128]{2,1,0:T(8,128)(2,1)}, u32[]{:S(2)}, u32[]{:S(2)}) collective-permute-start(bf16[16,128,128]{2,1,0:T(8,128)(2,1)} %fusion.72), channel_id=1, source_target_pairs={{0,64},{4,68},{8,72},{12,76},{16,80},{20,84},{24,88},{28,92},{32,9... | collective-permute-start | bytes 1572872 | tf_op jit(solution)/shard_map/ppermute | solution.py:15
  138.1 3.1 convolution_bitcast_fusion.1
  141.3 5.1 %multiply_reduce_fusion = (f32[128,16]{0,1:T(8,128)S(1)}, f32[128,16,128]{0,2,1:T(8,128)S(1)}) fusion(f32[128,16,128]{0,2,1:T(8,128)} %convolution_bitcast_fusion.1, f32[128,16]{0,1:T(8,128)S(1)} %get-tuple-element.14, bf16[16,128,128]{2,1,0:T(8,128)(2,1)} %collective-permute-done.5, f32[16]{0:T(128)} %get-tuple-element.8, ...), kind=kOutput, calls=%fused_computation.27 | convolution fusion | flops 408156160 | bytes 5783872 | tf_op jit(solution)/shard_map/ihd,hde->ihe/dot_general | solution.py:87
  158.4 9.3 %convolution_convert_fusion.1 = bf16[320,3072]{1,0:T(8,128)(2,1)S(1)} fusion(bf16[2048,3072]{0,1:T(8,128)(2,1)} %all-gather.3.cloned.1.call-done, bf16[160,2048]{1,0:T(8,128)(2,1)} %get-tuple-element.5, bf16[160,2048]{1,0:T(8,128)(2,1)} %get-tuple-element.4), kind=kOutput, calls=%fused_computation.1 | convolution fusion | flops 4030136320 | bytes 15859712 | tf_op jit(solution)/shard_map/dot_general | solution.py:119
  169.1 4.4 %all-to-all-start = ((bf16[2,4,40,3072]{3,2,0,1:T(8,128)(2,1)}), bf16[2,4,40,3072]{3,2,0,1:T(8,128)(2,1)}, u32[]{:S(2)}, u32[]{:S(2)}) async-start(bf16[2,4,40,3072]{3,2,0,1:T(8,128)(2,1)} %copy.57), calls=%async_computation | async-start | bytes 3932160 | tf_op jit(solution)/shard_map/all_to_all | solution.py:121
  176.1 23.0 %all-to-all-done = bf16[2,4,40,3072]{3,2,0,1:T(8,128)(2,1)} async-done(((bf16[2,4,40,3072]{3,2,0,1:T(8,128)(2,1)}), bf16[2,4,40,3072]{3,2,0,1:T(8,128)(2,1)}, u32[]{:S(2)}, u32[]{:S(2)}) %all-to-all-start) | async-done | bytes 1966112 | tf_op jit(solution)/shard_map/all_to_all | solution.py:121
  204.2 3.0 stack.10
  207.2 3.0 stack.9
  210.2 3.8 %maximum_bitcast_fusion = f32[40,16,2,192]{3,2,1,0:T(2,128)} fusion(f32[1,40,16,192]{3,0,2,1:T(1,128)} %stack.10, f32[1,40,16,192]{3,0,2,1:T(1,128)} %stack.9), kind=kLoop, calls=%fused_computation.21 | loop fusion | flops 245760 | bytes 1966080 | tf_op jit(solution)/shard_map/transpose | solution.py:130
  214.0 3.6 %reshape.214 = f32[40,6144]{1,0:T(8,128)} reshape(f32[40,16,2,192]{3,2,1,0:T(2,128)} %maximum_bitcast_fusion) | data formatting | bytes 1966080 | tf_op jit(solution)/shard_map/reshape | solution.py:131
  223.6 49.1 %all-gather.5.cloned.1.call-done = bf16[256,6144]{1,0:T(8,128)(2,1)} async-done(((bf16[16,6144]{1,0:T(8,128)(2,1)}), bf16[256,6144]{1,0:T(8,128)(2,1)}) %all-gather.5.cloned.1.call-update) | async-done | bytes 3145744 | tf_op jit(solution)/shard_map/all_gather | solution.py:143
  272.7 4.8 %fusion.3 = f32[256,288]{0,1:T(8,128)} fusion(bf16[256,6144]{1,0:T(8,128)(2,1)} %all-gather.5.cloned.1.call-done, bf16[1,6144,288]{1,2,0:T(8,128)(2,1)} %param.25), kind=kOutput, calls=%fused_computation.6 | convolution fusion | flops 905969664 | bytes 6979584 | tf_op jit(solution)/shard_map/dot_general | solution.py:144
  277.4 9.4 %convolution_convert_fusion = bf16[256,6144]{1,0:T(8,128)(2,1)} fusion(bf16[1,288,6144]{2,1,0:T(8,128)(2,1)S(1)} %copy-done, bf16[256,6144]{1,0:T(8,128)(2,1)} %all-gather.5.cloned.1.call-done, bf16[1,6144,288]{1,2,0:T(8,128)(2,1)} %param.26, f32[256,288]{0,1:T(8,128)} %fusion.3), kind=kOutput, calls=%fused_computation | convolution fusion | flops 1813954560 | bytes 13664256 | tf_op jit(solution)/shard_map/dot_general | solution.py:147
  288.7 3.4 %collective-permute-done.9 = bf16[16,8,6144]{2,1,0:T(8,128)(2,1)S(1)} collective-permute-done((bf16[16,8,6144]{2,1,0:T(8,128)(2,1)S(1)}, bf16[16,8,6144]{2,1,0:T(8,128)(2,1)S(1)}, u32[]{:S(2)}, u32[]{:S(2)}) %collective-permute-start.9) | collective-permute-done | bytes 1572896 | tf_op jit(solution)/shard_map/ppermute | solution.py:27
  293.6 4.5 %all-to-all-start.1 = ((bf16[16,8,6144]{2,1,0:T(8,128)(2,1)}), bf16[16,8,6144]{2,1,0:T(8,128)(2,1)}, u32[]{:S(2)}, u32[]{:S(2)}) async-start(bf16[16,8,6144]{2,1,0:T(8,128)(2,1)} %fusion.5), calls=%async_computation.1 | async-start | bytes 3145728 | tf_op jit(solution)/shard_map/all_to_all | solution.py:152
  300.0 22.7 %all-to-all-done.1 = bf16[16,8,6144]{2,1,0:T(8,128)(2,1)} async-done(((bf16[16,8,6144]{2,1,0:T(8,128)(2,1)}), bf16[16,8,6144]{2,1,0:T(8,128)(2,1)}, u32[]{:S(2)}, u32[]{:S(2)}) %all-to-all-start.1) | async-done | bytes 1572896 | tf_op jit(solution)/shard_map/all_to_all | solution.py:152
  (96 shorter events, 55.7 us)
Async XLA Ops:
  7.2 270.3 %copy-start = (bf16[1,288,6144]{2,1,0:T(8,128)(2,1)S(1)}, bf16[1,288,6144]{2,1,0:T(8,128)(2,1)}, u32[]{:S(2)}) copy-start(bf16[1,288,6144]{2,1,0:T(8,128)(2,1)} %param.27) | copy-start | bytes 10616836
  7.2 151.3 %all-gather.3.cloned.1.call-start = ((), (), s32[]{:S(2)}) async-start(), calls=%async_computation.2 | async-start | bytes 13369344 | tf_op jit(solution)/shard_map/all_gather | solution.py:117
  11.5 80.7 %copy-start.15 = (f32[16]{0:T(128)}, f32[16]{0:T(128)S(1)}, u32[]{:S(2)}) copy-start(f32[16]{0:T(128)S(1)} %get-tuple-element.13) | copy-start | bytes 196
  11.5 82.0 %copy-start.8 = (f32[16]{0:T(128)}, f32[16]{0:T(128)S(1)}, u32[]{:S(2)}) copy-start(f32[16]{0:T(128)S(1)} %get-tuple-element.10) | copy-start | bytes 196
  11.5 82.0 %copy-start.11 = (f32[16]{0:T(128)}, f32[16]{0:T(128)S(1)}, u32[]{:S(2)}) copy-start(f32[16]{0:T(128)S(1)} %get-tuple-element.11) | copy-start | bytes 196
  11.6 102.9 %copy-start.7 = (f32[16]{0:T(128)}, f32[16]{0:T(128)S(1)}, u32[]{:S(2)}) copy-start(f32[16]{0:T(128)S(1)} %get-tuple-element.9) | copy-start | bytes 196
  13.5 2.8 collective-permute-start
  16.3 77.2 %copy-start.1 = (bf16[16,128,128]{2,1,0:T(8,128)(2,1)}, bf16[16,128,128]{2,1,0:T(8,128)(2,1)S(1)}, u32[]{:S(2)}) copy-start(bf16[16,128,128]{2,1,0:T(8,128)(2,1)S(1)} %collective-permute-done) | copy-start | bytes 1572868
  16.3 10.7 %collective-permute-start.1 = (bf16[16,128,128]{2,1,0:T(8,128)(2,1)S(1)}, bf16[16,128,128]{2,1,0:T(8,128)(2,1)S(1)}, u32[]{:S(2)}, u32[]{:S(2)}) collective-permute-start(bf16[16,128,128]{2,1,0:T(8,128)(2,1)S(1)} %collective-permute-done), channel_id=1, source_target_pairs={{0,4},{4,8},{8,12},{12,16},{16,20},{20,24},{24,28},{28,32},{32,36}... | collective-permute-start | bytes 1572872 | tf_op jit(solution)/shard_map/ppermute | solution.py:15
  27.1 66.5 %copy-start.2 = (bf16[16,128,128]{2,1,0:T(8,128)(2,1)}, bf16[16,128,128]{2,1,0:T(8,128)(2,1)S(1)}, u32[]{:S(2)}) copy-start(bf16[16,128,128]{2,1,0:T(8,128)(2,1)S(1)} %collective-permute-done.1) | copy-start | bytes 1572868
  27.1 76.8 %copy-start.13 = (s32[128,2]{0,1:T(2,128)S(1)}, s32[128,2]{0,1:T(2,128)}, u32[]{:S(2)}) copy-start(s32[128,2]{0,1:T(2,128)} %param.23) | copy-start | bytes 3076
  27.3 37.2 %collective-permute-start.2 = (bf16[16,128,128]{2,1,0:T(8,128)(2,1)S(1)}, bf16[16,128,128]{2,1,0:T(8,128)(2,1)S(1)}, u32[]{:S(2)}, u32[]{:S(2)}) collective-permute-start(bf16[16,128,128]{2,1,0:T(8,128)(2,1)S(1)} %fusion.29), channel_id=1, source_target_pairs={{0,8},{4,12},{8,16},{12,20},{16,24},{20,28},{24,32},{28,36},{32,40... | collective-permute-start | bytes 1572872 | tf_op jit(solution)/shard_map/ppermute | solution.py:15
  64.6 39.3 %copy-start.4 = (bf16[16,128,128]{2,1,0:T(8,128)(2,1)}, bf16[16,128,128]{2,1,0:T(8,128)(2,1)S(1)}, u32[]{:S(2)}) copy-start(bf16[16,128,128]{2,1,0:T(8,128)(2,1)S(1)} %collective-permute-done.2) | copy-start | bytes 1572868
  65.0 27.2 %collective-permute-start.3 = (bf16[16,128,128]{2,1,0:T(8,128)(2,1)S(1)}, bf16[16,128,128]{2,1,0:T(8,128)(2,1)S(1)}, u32[]{:S(2)}, u32[]{:S(2)}) collective-permute-start(bf16[16,128,128]{2,1,0:T(8,128)(2,1)S(1)} %fusion.73), channel_id=1, source_target_pairs={{0,16},{4,20},{8,24},{12,28},{16,32},{20,36},{24,40},{28,44},{32,4... | collective-permute-start | bytes 1572872 | tf_op jit(solution)/shard_map/ppermute | solution.py:15
  92.2 11.6 %copy-start.5 = (bf16[16,128,128]{2,1,0:T(8,128)(2,1)}, bf16[16,128,128]{2,1,0:T(8,128)(2,1)S(1)}, u32[]{:S(2)}) copy-start(bf16[16,128,128]{2,1,0:T(8,128)(2,1)S(1)} %collective-permute-done.3) | copy-start | bytes 1572868
  93.6 20.8 %collective-permute-start.4 = (bf16[16,128,128]{2,1,0:T(8,128)(2,1)}, bf16[16,128,128]{2,1,0:T(8,128)(2,1)}, u32[]{:S(2)}, u32[]{:S(2)}) collective-permute-start(bf16[16,128,128]{2,1,0:T(8,128)(2,1)} %fusion.32), channel_id=1, source_target_pairs={{0,32},{4,36},{8,40},{12,44},{16,48},{20,52},{24,56},{28,60},{32,6... | collective-permute-start | bytes 1572872 | tf_op jit(solution)/shard_map/ppermute | solution.py:15
  117.5 23.7 %collective-permute-start.5 = (bf16[16,128,128]{2,1,0:T(8,128)(2,1)}, bf16[16,128,128]{2,1,0:T(8,128)(2,1)}, u32[]{:S(2)}, u32[]{:S(2)}) collective-permute-start(bf16[16,128,128]{2,1,0:T(8,128)(2,1)} %fusion.72), channel_id=1, source_target_pairs={{0,64},{4,68},{8,72},{12,76},{16,80},{20,84},{24,88},{28,92},{32,9... | collective-permute-start | bytes 1572872 | tf_op jit(solution)/shard_map/ppermute | solution.py:15
  153.5 2.4 collective-permute-start.6
  169.1 30.0 %all-to-all-start = ((bf16[2,4,40,3072]{3,2,0,1:T(8,128)(2,1)}), bf16[2,4,40,3072]{3,2,0,1:T(8,128)(2,1)}, u32[]{:S(2)}, u32[]{:S(2)}) async-start(bf16[2,4,40,3072]{3,2,0,1:T(8,128)(2,1)} %copy.57), calls=%async_computation | async-start | bytes 3932160 | tf_op jit(solution)/shard_map/all_to_all | solution.py:121
  173.6 99.1 %all-gather.5.cloned.1.call-start = ((), (), s32[]{:S(2)}) async-start(), calls=%async_computation.3 | async-start | bytes 3342336 | tf_op jit(solution)/shard_map/all_gather | solution.py:143
  201.2 2.0 collective-permute-start.7
  220.3 1.7 collective-permute-start.8
  288.6 3.5 %collective-permute-start.9 = (bf16[16,8,6144]{2,1,0:T(8,128)(2,1)S(1)}, bf16[16,8,6144]{2,1,0:T(8,128)(2,1)S(1)}, u32[]{:S(2)}, u32[]{:S(2)}) collective-permute-start(bf16[16,8,6144]{2,1,0:T(8,128)(2,1)S(1)} %dynamic-slice_bitcast_fusion), channel_id=1, source_target_pairs={{0,4},{4,0},{1,5},{5,1},{2,6},{6,2},{3,7},{7,3},{8,12},{12,8},{9,1... | collective-permute-start | bytes 4718600 | tf_op jit(solution)/shard_map/ppermute | solution.py:27
  293.6 29.1 %all-to-all-start.1 = ((bf16[16,8,6144]{2,1,0:T(8,128)(2,1)}), bf16[16,8,6144]{2,1,0:T(8,128)(2,1)}, u32[]{:S(2)}, u32[]{:S(2)}) async-start(bf16[16,8,6144]{2,1,0:T(8,128)(2,1)} %fusion.5), calls=%async_computation.1 | async-start | bytes 3145728 | tf_op jit(solution)/shard_map/all_to_all | solution.py:152
  (7 other events, 42.1 us)
Sparse Core Ops, SparseCore 0:
  10.2 109.4 all-gather.2
  223.7 48.9 all-gather.4

commit v5 on v4

--- a/solution.py
+++ b/solution.py
@@ -7,22 +7,6 @@
 CTX = ("yz", "core")
 
 
-def decayed_prefix(local_state, decay_rates, rows_here):
-    count = lax.axis_size(CTX)
-
-    def shift(value, step):
-        pairs = [(i, i + step) for i in range(count - step)]
-        return lax.ppermute(value.astype(jnp.bfloat16), CTX, pairs).astype(jnp.float32)
-
-    running = shift(local_state, 1)
-    step = 1
-    while step < count:
-        factor = jnp.exp(-decay_rates * (rows_here * step))
-        running = running + factor[:, None, None] * shift(running, step)
-        step *= 2
-    return running
-
-
 def partner(value):
     return lax.ppermute(value, "core", [(0, 1), (1, 0)])
 
@@ -30,6 +14,33 @@
 def by_core(mine, theirs):
     first = lax.axis_index("core") == 0
     return jnp.where(first, mine, theirs), jnp.where(first, theirs, mine)
+
+
+def decayed_prefix(local_state, decay_rates, rows_here):
+    chips = lax.axis_size("yz")
+    core_here = lax.axis_index("core")
+    half = local_state.shape[0] // 2
+    span = jnp.exp(-decay_rates * rows_here)
+    other = partner(local_state)
+    first_state, second_state = by_core(local_state, other)
+    chip_state = span[:, None, None] * first_state + second_state
+    my_rates = lax.dynamic_slice_in_dim(decay_rates, core_here * half, half, 0)
+    running = lax.dynamic_slice_in_dim(chip_state, core_here * half, half, 0)
+
+    def shift(value, step):
+        pairs = [(i, i + step) for i in range(chips - step)]
+        return lax.ppermute(value.astype(jnp.bfloat16), "yz", pairs).astype(jnp.float32)
+
+    running = shift(running, 1)
+    step = 1
+    while step < chips:
+        factor = jnp.exp(-my_rates * (2 * rows_here * step))
+        running = running + factor[:, None, None] * shift(running, step)
+        step *= 2
+    mine, theirs = running, partner(running)
+    low, high = by_core(mine, theirs)
+    chip_prefix = jnp.concatenate([low, high], axis=0)
+    return jnp.where(core_here == 0, chip_prefix, span[:, None, None] * chip_prefix + first_state)
 
 
 def normalize_rows(row_block, ffn_gain):

time: 333 us -> 300 us (0.901)
  starting transfers between devices: 73.1 us -> 39.4 us
    ppermute x6 -> x5, starting transfers between devices: 63.1 us -> 28.6 us  [shift(): lax.ppermute(value.astype(jnp.bfloat16), 'yz', pairs).astype(jnp.float32)]
    ppermute x6 -> x5, waiting for transfers between devices: 47.8 us -> 44.1 us  [shift(): lax.ppermute(value.astype(jnp.bfloat16), 'yz', pairs).astype(jnp.float32)]
    ppermute x4 -> x6, waiting for transfers between devices: 6.78 us -> 9 us  [partner(): return lax.ppermute(value, 'core', [(0, 1), (1, 0)])]
  transfers between devices with their start and end apart: 14 -> 15, of which waited for: 11 -> 12; matrix products, arithmetic and copies ran while one was open for 13% -> 15% of each run, Pallas kernels for 0% -> 0%
where the time goes in v5:
time: 300 us; the launch traced here: 298 us
  waiting for transfers between devices  148 us (49%)
  starting transfers between devices  39.4 us (13%)
  matrix products  36.7 us (12%)
  other arithmetic  35.2 us (12%)
  local copies, waits for them, and re-layouts  24.8 us (8%)
  between operations  14.3 us (5%)
    all_gather x1, waiting for transfers between devices, per_device(): row_piece = lax.all_gather(chip_rows, 'yz', axis=0, tiled=True)  48.3 us
    ppermute x5, waiting for transfers between devices, shift(): lax.ppermute(value.astype(jnp.bfloat16), 'yz', pairs).astype(jnp.float32)  44.1 us
    ppermute x5, starting transfers between devices, shift(): lax.ppermute(value.astype(jnp.bfloat16), 'yz', pairs).astype(jnp.float32)  28.6 us
    all_to_all x1, waiting for transfers between devices, per_device(): swapped = lax.all_to_all(partial_term, 'exp', 1, 1, tiled=True)  23.2 us
    all_to_all x1, waiting for transfers between devices, per_device(): lax.all_to_all(pair_sum.astype(jnp.bfloat16), 'yz', 0, 0, tiled=True)  22.6 us
    dot_general x1, matrix products, per_device(): jnp.dot(activated, w_down[0], preferred_element_type=jnp.float32)  9.41 us
    dot_general x1, matrix products, per_device(): jnp.dot(pair_rows, half_weight, preferred_element_type=jnp.float32)  9.25 us
    ppermute x6, waiting for transfers between devices, partner(): return lax.ppermute(value, 'core', [(0, 1), (1, 0)])  9 us
  transfers between devices with their start and end apart: 15, of which 12 were waited for; matrix products, arithmetic and copies ran while one was open for 15% of the time, Pallas kernels for 0%

profile of v5, /device:TPU:0, one launch (start us, length us, event | category | flops | bytes accessed | tf_op | source)
XLA Modules:
  0.0 298.5 jit_solution(14931519930825006208)
XLA Ops:
  21.2 3.9 %collective-permute-start.1 = (bf16[8,128,128]{2,1,0:T(8,128)(2,1)S(1)}, bf16[8,128,128]{2,1,0:T(8,128)(2,1)S(1)}, u32[]{:S(2)}, u32[]{:S(2)}) collective-permute-start(bf16[8,128,128]{2,1,0:T(8,128)(2,1)S(1)} %fusion.38), channel_id=1, source_target_pairs={{0,8},{8,16},{16,24},{24,32},{32,40},{40,48},{48,56},{56,64},{64,7... | collective-permute-start | bytes 786440 | tf_op jit(solution)/shard_map/ppermute | solution.py:32
  25.2 11.9 %collective-permute-done.1 = bf16[8,128,128]{2,1,0:T(8,128)(2,1)S(1)} collective-permute-done((bf16[8,128,128]{2,1,0:T(8,128)(2,1)S(1)}, bf16[8,128,128]{2,1,0:T(8,128)(2,1)S(1)}, u32[]{:S(2)}, u32[]{:S(2)}) %collective-permute-start.1) | collective-permute-done | bytes 262176 | tf_op jit(solution)/shard_map/ppermute | solution.py:32
  37.1 4.4 %collective-permute-start.2 = (bf16[8,128,128]{2,1,0:T(8,128)(2,1)S(1)}, bf16[8,128,128]{2,1,0:T(8,128)(2,1)S(1)}, u32[]{:S(2)}, u32[]{:S(2)}) collective-permute-start(bf16[8,128,128]{2,1,0:T(8,128)(2,1)S(1)} %collective-permute-done.1), channel_id=1, source_target_pairs={{0,8},{8,16},{16,24},{24,32},{32,40},{40,48},{48,56},{56,64},{64,7... | collective-permute-start | bytes 786440 | tf_op jit(solution)/shard_map/ppermute | solution.py:32
  42.2 5.5 %collective-permute-done.2 = bf16[8,128,128]{2,1,0:T(8,128)(2,1)S(1)} collective-permute-done((bf16[8,128,128]{2,1,0:T(8,128)(2,1)S(1)}, bf16[8,128,128]{2,1,0:T(8,128)(2,1)S(1)}, u32[]{:S(2)}, u32[]{:S(2)}) %collective-permute-start.2) | collective-permute-done | bytes 262176 | tf_op jit(solution)/shard_map/ppermute | solution.py:32
  47.8 6.2 %collective-permute-start.3 = (bf16[8,128,128]{2,1,0:T(8,128)(2,1)S(1)}, bf16[8,128,128]{2,1,0:T(8,128)(2,1)S(1)}, u32[]{:S(2)}, u32[]{:S(2)}) collective-permute-start(bf16[8,128,128]{2,1,0:T(8,128)(2,1)S(1)} %fusion.47), channel_id=1, source_target_pairs={{0,16},{8,24},{16,32},{24,40},{32,48},{40,56},{48,64},{56,72},{64,... | collective-permute-start | bytes 786440 | tf_op jit(solution)/shard_map/ppermute | solution.py:32
  54.0 11.0 %collective-permute-done.3 = bf16[8,128,128]{2,1,0:T(8,128)(2,1)S(1)} collective-permute-done((bf16[8,128,128]{2,1,0:T(8,128)(2,1)S(1)}, bf16[8,128,128]{2,1,0:T(8,128)(2,1)S(1)}, u32[]{:S(2)}, u32[]{:S(2)}) %collective-permute-start.3) | collective-permute-done | bytes 262176 | tf_op jit(solution)/shard_map/ppermute | solution.py:32
  65.3 7.1 %collective-permute-start.4 = (bf16[8,128,128]{2,1,0:T(8,128)(2,1)S(1)}, bf16[8,128,128]{2,1,0:T(8,128)(2,1)S(1)}, u32[]{:S(2)}, u32[]{:S(2)}) collective-permute-start(bf16[8,128,128]{2,1,0:T(8,128)(2,1)S(1)} %fusion.77), channel_id=1, source_target_pairs={{0,32},{8,40},{16,48},{24,56},{32,64},{40,72},{48,80},{56,88},{64,... | collective-permute-start | bytes 786440 | tf_op jit(solution)/shard_map/ppermute | solution.py:32
  73.1 9.7 %collective-permute-done.4 = bf16[8,128,128]{2,1,0:T(8,128)(2,1)S(1)} collective-permute-done((bf16[8,128,128]{2,1,0:T(8,128)(2,1)S(1)}, bf16[8,128,128]{2,1,0:T(8,128)(2,1)S(1)}, u32[]{:S(2)}, u32[]{:S(2)}) %collective-permute-start.4) | collective-permute-done | bytes 262176 | tf_op jit(solution)/shard_map/ppermute | solution.py:32
  83.8 6.9 %collective-permute-start.5 = (bf16[8,128,128]{2,1,0:T(8,128)(2,1)}, bf16[8,128,128]{2,1,0:T(8,128)(2,1)}, u32[]{:S(2)}, u32[]{:S(2)}) collective-permute-start(bf16[8,128,128]{2,1,0:T(8,128)(2,1)} %fusion.53), channel_id=1, source_target_pairs={{0,64},{8,72},{16,80},{24,88},{32,96},{40,104},{48,112},{56,120},{... | collective-permute-start | bytes 786440 | tf_op jit(solution)/shard_map/ppermute | solution.py:32
  94.7 6.0 %collective-permute-done.5 = bf16[8,128,128]{2,1,0:T(8,128)(2,1)} collective-permute-done((bf16[8,128,128]{2,1,0:T(8,128)(2,1)}, bf16[8,128,128]{2,1,0:T(8,128)(2,1)}, u32[]{:S(2)}, u32[]{:S(2)}) %collective-permute-start.5) | collective-permute-done | bytes 262176 | tf_op jit(solution)/shard_map/ppermute | solution.py:32
  107.1 3.1 %convolution_bitcast_fusion.1 = f32[128,16,128]{0,2,1:T(8,128)} fusion(bf16[128,16,128]{0,2,1:T(8,128)(2,1)} %bitcast.99, f32[128,128]{1,0:T(8,128)} %fusion.64, f32[16]{0:T(128)} %copy-done.16, pred[128,128]{1,0:T(8,128)(4,1)} %fusion.65, bf16[128,2048]{1,0:T(8,128)(2,1)} %param.17, bf16[128,2048]{1,0:T(8,128)(2,1)} %param.15), kind=kOutput, calls=%fused_computation.16 | convolution fusion | flops 135266304 | bytes 2703424 | tf_op jit(solution)/shard_map/hij,jhd->ihd/dot_general | solution.py:94
  111.5 4.0 %multiply_reduce_fusion = (f32[128,16]{0,1:T(8,128)S(1)}, f32[128,16,128]{0,2,1:T(8,128)S(1)}) fusion(f32[128,16,128]{0,2,1:T(8,128)} %convolution_bitcast_fusion.1, f32[128,16]{0,1:T(8,128)S(1)} %get-tuple-element.12, f32[16,128,128]{2,1,0:T(8,128)} %copy-done.2, f32[8,128,128]{2,1,0:T(8,128)S(1)} %get-tuple-element.9, ...), kind=kOutput, calls=%fused_computation.27 | convolution fusion | flops 405010432 | bytes 4735041 | tf_op jit(solution)/shard_map/ihd,hde->ihe/dot_general | solution.py:98
  125.5 9.3 %convolution_convert_fusion.1 = bf16[320,3072]{1,0:T(8,128)(2,1)S(1)} fusion(bf16[2048,3072]{0,1:T(8,128)(2,1)} %all-gather.3.cloned.1.call-done, bf16[160,2048]{1,0:T(8,128)(2,1)} %get-tuple-element.7, bf16[160,2048]{1,0:T(8,128)(2,1)} %get-tuple-element.6), kind=kOutput, calls=%fused_computation.1 | convolution fusion | flops 4030136320 | bytes 15859712 | tf_op jit(solution)/shard_map/dot_general | solution.py:130
  136.2 4.5 %all-to-all-start = ((bf16[2,4,40,3072]{3,2,0,1:T(8,128)(2,1)}), bf16[2,4,40,3072]{3,2,0,1:T(8,128)(2,1)}, u32[]{:S(2)}, u32[]{:S(2)}) async-start(bf16[2,4,40,3072]{3,2,0,1:T(8,128)(2,1)} %copy.57), calls=%async_computation | async-start | bytes 3932160 | tf_op jit(solution)/shard_map/all_to_all | solution.py:132
  143.2 23.2 %all-to-all-done = bf16[2,4,40,3072]{3,2,0,1:T(8,128)(2,1)} async-done(((bf16[2,4,40,3072]{3,2,0,1:T(8,128)(2,1)}), bf16[2,4,40,3072]{3,2,0,1:T(8,128)(2,1)}, u32[]{:S(2)}, u32[]{:S(2)}) %all-to-all-start) | async-done | bytes 1966112 | tf_op jit(solution)/shard_map/all_to_all | solution.py:132
  171.6 3.0 %stack.10 = f32[1,40,16,192]{3,0,2,1:T(1,128)} reshape(f32[40,3072]{1,0:T(8,128)} %get-tuple-element.5) | data formatting | bytes 983040 | tf_op jit(solution)/shard_map/stack | solution.py:137
  177.6 3.8 %maximum_bitcast_fusion = f32[40,16,2,192]{3,2,1,0:T(2,128)} fusion(f32[1,40,16,192]{3,0,2,1:T(1,128)} %stack.10, f32[1,40,16,192]{3,0,2,1:T(1,128)} %stack.9), kind=kLoop, calls=%fused_computation.21 | loop fusion | flops 245760 | bytes 1966080 | tf_op jit(solution)/shard_map/transpose | solution.py:141
  181.4 3.6 %reshape.214 = f32[40,6144]{1,0:T(8,128)} reshape(f32[40,16,2,192]{3,2,1,0:T(2,128)} %maximum_bitcast_fusion) | data formatting | bytes 1966080 | tf_op jit(solution)/shard_map/reshape | solution.py:142
  191.0 48.3 %all-gather.5.cloned.1.call-done = bf16[256,6144]{1,0:T(8,128)(2,1)} async-done(((bf16[16,6144]{1,0:T(8,128)(2,1)}), bf16[256,6144]{1,0:T(8,128)(2,1)}) %all-gather.5.cloned.1.call-update) | async-done | bytes 3145744 | tf_op jit(solution)/shard_map/all_gather | solution.py:154
  239.3 4.8 %fusion.3 = f32[256,288]{0,1:T(8,128)} fusion(bf16[256,6144]{1,0:T(8,128)(2,1)} %all-gather.5.cloned.1.call-done, bf16[1,6144,288]{1,2,0:T(8,128)(2,1)} %param.25), kind=kOutput, calls=%fused_computation.6 | convolution fusion | flops 905969664 | bytes 6979584 | tf_op jit(solution)/shard_map/dot_general | solution.py:155
  244.1 9.4 %convolution_convert_fusion = bf16[256,6144]{1,0:T(8,128)(2,1)} fusion(bf16[1,288,6144]{2,1,0:T(8,128)(2,1)S(1)} %copy-done, bf16[256,6144]{1,0:T(8,128)(2,1)} %all-gather.5.cloned.1.call-done, bf16[1,6144,288]{1,2,0:T(8,128)(2,1)} %param.26, f32[256,288]{0,1:T(8,128)} %fusion.3), kind=kOutput, calls=%fused_computation | convolution fusion | flops 1813954560 | bytes 13664256 | tf_op jit(solution)/shard_map/dot_general | solution.py:158
  255.3 3.4 %collective-permute-done.10 = bf16[16,8,6144]{2,1,0:T(8,128)(2,1)S(1)} collective-permute-done((bf16[16,8,6144]{2,1,0:T(8,128)(2,1)S(1)}, bf16[16,8,6144]{2,1,0:T(8,128)(2,1)S(1)}, u32[]{:S(2)}, u32[]{:S(2)}) %collective-permute-start.10) | collective-permute-done | bytes 1572896 | tf_op jit(solution)/shard_map/ppermute | solution.py:11
  260.2 4.5 %all-to-all-start.1 = ((bf16[16,8,6144]{2,1,0:T(8,128)(2,1)}), bf16[16,8,6144]{2,1,0:T(8,128)(2,1)}, u32[]{:S(2)}, u32[]{:S(2)}) async-start(bf16[16,8,6144]{2,1,0:T(8,128)(2,1)} %fusion.5), calls=%async_computation.1 | async-start | bytes 3145728 | tf_op jit(solution)/shard_map/all_to_all | solution.py:163
  266.6 22.6 %all-to-all-done.1 = bf16[16,8,6144]{2,1,0:T(8,128)(2,1)} async-done(((bf16[16,8,6144]{2,1,0:T(8,128)(2,1)}), bf16[16,8,6144]{2,1,0:T(8,128)(2,1)}, u32[]{:S(2)}, u32[]{:S(2)}) %all-to-all-start.1) | async-done | bytes 1572896 | tf_op jit(solution)/shard_map/all_to_all | solution.py:163
  (108 shorter events, 63.9 us)
Async XLA Ops:
  7.2 236.9 %copy-start = (bf16[1,288,6144]{2,1,0:T(8,128)(2,1)S(1)}, bf16[1,288,6144]{2,1,0:T(8,128)(2,1)}, u32[]{:S(2)}) copy-start(bf16[1,288,6144]{2,1,0:T(8,128)(2,1)} %param.27) | copy-start | bytes 10616836
  7.2 118.3 %all-gather.3.cloned.1.call-start = ((), (), s32[]{:S(2)}) async-start(), calls=%async_computation.2 | async-start | bytes 13369344 | tf_op jit(solution)/shard_map/all_gather | solution.py:128
  11.0 10.3 %copy-start.18 = (f32[16]{0:T(128)}, f32[16]{0:T(128)S(1)}, u32[]{:S(2)}) copy-start(f32[16]{0:T(128)S(1)} %get-tuple-element.17) | copy-start | bytes 196
  11.6 29.8 %copy-start.17 = (f32[16]{0:T(128)S(1)}, f32[16]{0:T(128)}, u32[]{:S(2)}) copy-start(f32[16]{0:T(128)} %param.19) | copy-start | bytes 196
  14.5 3.0 %collective-permute-start = (f32[16,128,128]{2,1,0:T(8,128)}, f32[16,128,128]{2,1,0:T(8,128)}, u32[]{:S(2)}, u32[]{:S(2)}) collective-permute-start(f32[16,128,128]{2,1,0:T(8,128)} %fusion.23), channel_id=1, source_target_pairs={{0,4},{4,0},{1,5},{5,1},{2,6},{6,2},{3,7},{7,3},{8,12},{12,8},{9,1... | collective-permute-start | bytes 3145736 | tf_op jit(solution)/shard_map/ppermute | solution.py:11
  19.9 70.9 %copy-start.13 = (s32[128,2]{0,1:T(2,128)S(1)}, s32[128,2]{0,1:T(2,128)}, u32[]{:S(2)}) copy-start(s32[128,2]{0,1:T(2,128)} %param.23) | copy-start | bytes 3076
  21.2 15.8 %collective-permute-start.1 = (bf16[8,128,128]{2,1,0:T(8,128)(2,1)S(1)}, bf16[8,128,128]{2,1,0:T(8,128)(2,1)S(1)}, u32[]{:S(2)}, u32[]{:S(2)}) collective-permute-start(bf16[8,128,128]{2,1,0:T(8,128)(2,1)S(1)} %fusion.38), channel_id=1, source_target_pairs={{0,8},{8,16},{16,24},{24,32},{32,40},{40,48},{48,56},{56,64},{64,7... | collective-permute-start | bytes 786440 | tf_op jit(solution)/shard_map/ppermute | solution.py:32
  37.1 45.7 %copy-start.3 = (bf16[8,128,128]{2,1,0:T(8,128)(2,1)}, bf16[8,128,128]{2,1,0:T(8,128)(2,1)S(1)}, u32[]{:S(2)}) copy-start(bf16[8,128,128]{2,1,0:T(8,128)(2,1)S(1)} %collective-permute-done.1) | copy-start | bytes 786436
  37.1 10.6 %collective-permute-start.2 = (bf16[8,128,128]{2,1,0:T(8,128)(2,1)S(1)}, bf16[8,128,128]{2,1,0:T(8,128)(2,1)S(1)}, u32[]{:S(2)}, u32[]{:S(2)}) collective-permute-start(bf16[8,128,128]{2,1,0:T(8,128)(2,1)S(1)} %collective-permute-done.1), channel_id=1, source_target_pairs={{0,8},{8,16},{16,24},{24,32},{32,40},{40,48},{48,56},{56,64},{64,7... | collective-permute-start | bytes 786440 | tf_op jit(solution)/shard_map/ppermute | solution.py:32
  42.2 48.6 %copy-start.8 = (f32[8]{0:T(128)}, f32[8]{0:T(128)S(1)}, u32[]{:S(2)}) copy-start(f32[8]{0:T(128)S(1)} %get-tuple-element.15) | copy-start | bytes 100
  42.2 48.6 %copy-start.11 = (f32[8]{0:T(128)}, f32[8]{0:T(128)S(1)}, u32[]{:S(2)}) copy-start(f32[8]{0:T(128)S(1)} %get-tuple-element.14) | copy-start | bytes 100
  47.6 36.2 %copy-start.4 = (bf16[8,128,128]{2,1,0:T(8,128)(2,1)}, bf16[8,128,128]{2,1,0:T(8,128)(2,1)S(1)}, u32[]{:S(2)}) copy-start(bf16[8,128,128]{2,1,0:T(8,128)(2,1)S(1)} %collective-permute-done.2) | copy-start | bytes 786436
  47.8 17.2 %collective-permute-start.3 = (bf16[8,128,128]{2,1,0:T(8,128)(2,1)S(1)}, bf16[8,128,128]{2,1,0:T(8,128)(2,1)S(1)}, u32[]{:S(2)}, u32[]{:S(2)}) collective-permute-start(bf16[8,128,128]{2,1,0:T(8,128)(2,1)S(1)} %fusion.47), channel_id=1, source_target_pairs={{0,16},{8,24},{16,32},{24,40},{32,48},{40,56},{48,64},{56,72},{64,... | collective-permute-start | bytes 786440 | tf_op jit(solution)/shard_map/ppermute | solution.py:32
  65.0 25.7 %copy-start.6 = (bf16[8,128,128]{2,1,0:T(8,128)(2,1)}, bf16[8,128,128]{2,1,0:T(8,128)(2,1)S(1)}, u32[]{:S(2)}) copy-start(bf16[8,128,128]{2,1,0:T(8,128)(2,1)S(1)} %collective-permute-done.3) | copy-start | bytes 786436
  65.3 17.5 %collective-permute-start.4 = (bf16[8,128,128]{2,1,0:T(8,128)(2,1)S(1)}, bf16[8,128,128]{2,1,0:T(8,128)(2,1)S(1)}, u32[]{:S(2)}, u32[]{:S(2)}) collective-permute-start(bf16[8,128,128]{2,1,0:T(8,128)(2,1)S(1)} %fusion.77), channel_id=1, source_target_pairs={{0,32},{8,40},{16,48},{24,56},{32,64},{40,72},{48,80},{56,88},{64,... | collective-permute-start | bytes 786440 | tf_op jit(solution)/shard_map/ppermute | solution.py:32
  83.8 16.8 %collective-permute-start.5 = (bf16[8,128,128]{2,1,0:T(8,128)(2,1)}, bf16[8,128,128]{2,1,0:T(8,128)(2,1)}, u32[]{:S(2)}, u32[]{:S(2)}) collective-permute-start(bf16[8,128,128]{2,1,0:T(8,128)(2,1)} %fusion.53), channel_id=1, source_target_pairs={{0,64},{8,72},{16,80},{24,88},{32,96},{40,104},{48,112},{56,120},{... | collective-permute-start | bytes 786440 | tf_op jit(solution)/shard_map/ppermute | solution.py:32
  103.1 7.1 %collective-permute-start.6 = (f32[8,128,128]{2,1,0:T(8,128)}, f32[8,128,128]{2,1,0:T(8,128)}, u32[]{:S(2)}, u32[]{:S(2)}) collective-permute-start(f32[8,128,128]{2,1,0:T(8,128)} %multiply_add_fusion), channel_id=1, source_target_pairs={{0,4},{4,0},{1,5},{5,1},{2,6},{6,2},{3,7},{7,3},{8,12},{12,8},{9,1... | collective-permute-start | bytes 1572872 | tf_op jit(solution)/shard_map/ppermute | solution.py:11
  121.8 2.5 collective-permute-start.7
  136.2 30.2 %all-to-all-start = ((bf16[2,4,40,3072]{3,2,0,1:T(8,128)(2,1)}), bf16[2,4,40,3072]{3,2,0,1:T(8,128)(2,1)}, u32[]{:S(2)}, u32[]{:S(2)}) async-start(bf16[2,4,40,3072]{3,2,0,1:T(8,128)(2,1)} %copy.57), calls=%async_computation | async-start | bytes 3932160 | tf_op jit(solution)/shard_map/all_to_all | solution.py:132
  140.7 98.5 %all-gather.5.cloned.1.call-start = ((), (), s32[]{:S(2)}) async-start(), calls=%async_computation.3 | async-start | bytes 3342336 | tf_op jit(solution)/shard_map/all_gather | solution.py:154
  168.5 2.0 collective-permute-start.8
  187.6 1.7 collective-permute-start.9
  255.2 3.5 %collective-permute-start.10 = (bf16[16,8,6144]{2,1,0:T(8,128)(2,1)S(1)}, bf16[16,8,6144]{2,1,0:T(8,128)(2,1)S(1)}, u32[]{:S(2)}, u32[]{:S(2)}) collective-permute-start(bf16[16,8,6144]{2,1,0:T(8,128)(2,1)S(1)} %dynamic-slice_bitcast_fusion), channel_id=1, source_target_pairs={{0,4},{4,0},{1,5},{5,1},{2,6},{6,2},{3,7},{7,3},{8,12},{12,8},{9,1... | collective-permute-start | bytes 4718600 | tf_op jit(solution)/shard_map/ppermute | solution.py:11
  260.2 29.1 %all-to-all-start.1 = ((bf16[16,8,6144]{2,1,0:T(8,128)(2,1)}), bf16[16,8,6144]{2,1,0:T(8,128)(2,1)}, u32[]{:S(2)}, u32[]{:S(2)}) async-start(bf16[16,8,6144]{2,1,0:T(8,128)(2,1)} %fusion.5), calls=%async_computation.1 | async-start | bytes 3145728 | tf_op jit(solution)/shard_map/all_to_all | solution.py:163
  (10 other events, 51.7 us)
Sparse Core Ops, SparseCore 0:
  10.2 105.8 all-gather.2
  191.1 48.1 all-gather.4

commit v6 on v5

--- a/solution.py
+++ b/solution.py
@@ -119,39 +119,49 @@
     slot_mixed = jnp.dot(selector, mixed_heads, preferred_element_type=jnp.float32).astype(
         jnp.bfloat16
     )
-    row_blocks = jnp.concatenate(
-        [mixed_heads.reshape(exp_count, own_rows, -1), slot_mixed.reshape(exp_count, capacity, -1)],
-        axis=1,
-    )
-    stacked = row_blocks.reshape(exp_count * per_block, head_count * head_size)
-    pair_rows = jnp.concatenate(by_core(stacked, partner(stacked)), axis=0)
+    core_here = lax.axis_index("core")
+    block_width = out_weight.shape[1]
     half_weight = lax.all_gather(out_weight, "yz", axis=1, tiled=True)
     half_width = half_weight.shape[1]
-    partial_rows = jnp.dot(pair_rows, half_weight, preferred_element_type=jnp.float32)
-    partial_term = partial_rows.astype(jnp.bfloat16).reshape(2, exp_count, per_block, half_width)
-    swapped = lax.all_to_all(partial_term, "exp", 1, 1, tiled=True)
-    head_sum = jnp.sum(swapped.astype(jnp.float32), axis=1)
-    core_here = lax.axis_index("core")
-    kept = lax.dynamic_index_in_dim(head_sum, core_here, 0, keepdims=False)
-    sent = lax.dynamic_index_in_dim(head_sum, 1 - core_here, 0, keepdims=False)
-    by_parity = jnp.stack(by_core(kept, partner(sent)), axis=0)
-    block_width = out_weight.shape[1]
-    projected = (
-        by_parity.reshape(2, per_block, half_width // block_width, block_width)
-        .transpose(1, 2, 0, 3)
-        .reshape(per_block, model_width)
-    )
     stream_own = lax.dynamic_slice_in_dim(stream_in, own_index * own_rows, own_rows, 0)
     own_selector = lax.dynamic_slice_in_dim(selector, own_index * capacity, capacity, 0)
-    stream_slots = jnp.dot(own_selector, stream_in, preferred_element_type=jnp.float32)
-    residual_rows = jnp.concatenate([stream_own.astype(jnp.float32), stream_slots], axis=0)
-    hidden_rows = (residual_rows + projected).astype(jnp.bfloat16)
-    residual_out = hidden_rows[:own_rows]
-    slot_hidden = hidden_rows[own_rows:]
+    stream_slots = jnp.dot(own_selector, stream_in, preferred_element_type=jnp.float32).astype(
+        jnp.bfloat16
+    )
+
+    def parity_half(rows, parity):
+        shaped = rows.reshape(rows.shape[0], half_width // block_width, 2, block_width)
+        return lax.dynamic_index_in_dim(shaped, parity, 2, keepdims=False).reshape(
+            rows.shape[0], half_width
+        )
+
+    def project(row_block, stream_rows, count):
+        pair = jnp.concatenate(by_core(row_block, partner(row_block)), axis=0)
+        part = jnp.dot(pair, half_weight, preferred_element_type=jnp.float32)
+        part = part.astype(jnp.bfloat16).reshape(2, exp_count, count, half_width)
+        head_sum = jnp.sum(lax.all_to_all(part, "exp", 1, 1, tiled=True).astype(jnp.float32), axis=1)
+        stream_pair = by_core(
+            parity_half(stream_rows, core_here), partner(parity_half(stream_rows, 1 - core_here))
+        )
+        hidden_half = (jnp.stack(stream_pair, axis=0).astype(jnp.float32) + head_sum).astype(
+            jnp.bfloat16
+        )
+        kept = lax.dynamic_index_in_dim(hidden_half, core_here, 0, keepdims=False)
+        sent = lax.dynamic_index_in_dim(hidden_half, 1 - core_here, 0, keepdims=False)
+        low, high = by_core(kept, partner(sent))
+        shape = (count, half_width // block_width, 1, block_width)
+        return jnp.concatenate([low.reshape(shape), high.reshape(shape)], axis=2).reshape(
+            count, model_width
+        )
+
+    slot_hidden = project(slot_mixed, stream_slots, capacity)
+    residual_out = project(mixed_heads, stream_own, own_rows)
     outgoing = normalize_rows(slot_hidden, ffn_gain)
     ctx_count = lax.axis_size(CTX)
-    chip_rows = jnp.concatenate(by_core(outgoing, partner(outgoing)), axis=0)
-    row_piece = lax.all_gather(chip_rows, "yz", axis=0, tiled=True)
+    gathered = lax.all_gather(outgoing, "yz", axis=0, tiled=False)
+    row_piece = jnp.stack(by_core(gathered, partner(gathered)), axis=1).reshape(
+        ctx_count * capacity, model_width
+    )
     gate_part = jnp.dot(row_piece, w_gate[0], preferred_element_type=jnp.float32)
     up_part = jnp.dot(row_piece, w_up[0], preferred_element_type=jnp.float32)
     activated = (jax.nn.silu(gate_part) * up_part).astype(jnp.bfloat16)

time: 300 us -> 313 us (1.043)
  waiting for transfers between devices: 148 us -> 112 us
  local copies, waits for them, and re-layouts: 24.8 us -> 51 us
  other arithmetic: 35.2 us -> 46.3 us
  starting transfers between devices: 39.4 us -> 46.3 us
  matrix products: 36.7 us -> 41.8 us
    reshape x2 -> x13, local copies, waits for them, and re-layouts: 5.05 us -> 22.8 us  [the longest x4 6.99 us: parity_half(): lax.dynamic_index_in_dim(shaped, parity, 2, keepdims=False)]
    all_to_all x1 -> x2, waiting for transfers between devices: 23.2 us -> 7.48 us  [project(): lax.all_to_all(part, 'exp', 1, 1, tiled=True).astype(jnp.float32)]
    all_to_all x1, waiting for transfers between devices: 22.6 us -> 12.9 us  [per_device(): lax.all_to_all(pair_sum.astype(jnp.bfloat16), 'yz', 0, 0, tiled=True)]
    dynamic_slice x0 -> x3, local copies, waits for them, and re-layouts: none -> 9.54 us  [the longest x2 7.77 us: parity_half(): lax.dynamic_index_in_dim(shaped, parity, 2, keepdims=False)]
    all_gather x1, waiting for transfers between devices: 48.3 us -> 42 us  [per_device(): gathered = lax.all_gather(outgoing, 'yz', axis=0, tiled=False)]
    another operation x2 -> x0, local copies, waits for them, and re-layouts: 6.02 us -> none  [per_device(): by_parity = jnp.stack(by_core(kept, partner(sent)), axis=0)]
    another operation x0 -> x4, other arithmetic: none -> 5.65 us  [the longest x2 3.27 us: project(): jnp.stack(stream_pair, axis=0).astype(jnp.float32) + head_sum]
    dot_general x2 -> x3, matrix products: 14 us -> 18.5 us  [the longest x2 16.7 us: project(): part = jnp.dot(pair, half_weight, preferred_element_type=jnp.float32)]
  transfers between devices with their start and end apart: 15 -> 20, of which waited for: 12 -> 11; matrix products, arithmetic and copies ran while one was open for 15% -> 37% of each run, Pallas kernels for 0% -> 0%
where the time goes in v6:
time: 313 us; the launch traced here: 311 us
  waiting for transfers between devices  112 us (36%)
  local copies, waits for them, and re-layouts  51 us (16%)
  starting transfers between devices  46.3 us (15%)
  other arithmetic  46.3 us (15%)
  matrix products  41.8 us (13%)
  between operations  14.3 us (5%)
    ppermute x5, waiting for transfers between devices, shift(): lax.ppermute(value.astype(jnp.bfloat16), 'yz', pairs).astype(jnp.float32)  43.8 us
    all_gather x1, waiting for transfers between devices, per_device(): gathered = lax.all_gather(outgoing, 'yz', axis=0, tiled=False)  42 us
    ppermute x5, starting transfers between devices, shift(): lax.ppermute(value.astype(jnp.bfloat16), 'yz', pairs).astype(jnp.float32)  30.7 us
    dot_general x2, matrix products, project(): part = jnp.dot(pair, half_weight, preferred_element_type=jnp.float32)  16.7 us
    all_to_all x1, waiting for transfers between devices, per_device(): lax.all_to_all(pair_sum.astype(jnp.bfloat16), 'yz', 0, 0, tiled=True)  12.9 us
    dot_general x1, matrix products, per_device(): jnp.dot(activated, w_down[0], preferred_element_type=jnp.float32)  9.4 us
    all_to_all x2, starting transfers between devices, project(): lax.all_to_all(part, 'exp', 1, 1, tiled=True).astype(jnp.float32)  8.83 us
    dynamic_slice x2, local copies, waits for them, and re-layouts, parity_half(): lax.dynamic_index_in_dim(shaped, parity, 2, keepdims=False)  7.77 us
  transfers between devices with their start and end apart: 20, of which 11 were waited for; matrix products, arithmetic and copies ran while one was open for 37% of the time, Pallas kernels for 0%

profile of v6, /device:TPU:0, one launch (start us, length us, event | category | flops | bytes accessed | tf_op | source)
XLA Modules:
  0.0 311.2 jit_solution(7924870916413668210)
XLA Ops:
  12.2 2.9 fusion.16
  21.8 4.0 %collective-permute-start.2 = (bf16[8,128,128]{2,1,0:T(8,128)(2,1)S(1)}, bf16[8,128,128]{2,1,0:T(8,128)(2,1)S(1)}, u32[]{:S(2)}, u32[]{:S(2)}) collective-permute-start(bf16[8,128,128]{2,1,0:T(8,128)(2,1)S(1)} %fusion.28), channel_id=1, source_target_pairs={{0,8},{8,16},{16,24},{24,32},{32,40},{40,48},{48,56},{56,64},{64,7... | collective-permute-start | bytes 786440 | tf_op jit(solution)/shard_map/ppermute | solution.py:32
  25.8 11.9 %collective-permute-done.2 = bf16[8,128,128]{2,1,0:T(8,128)(2,1)S(1)} collective-permute-done((bf16[8,128,128]{2,1,0:T(8,128)(2,1)S(1)}, bf16[8,128,128]{2,1,0:T(8,128)(2,1)S(1)}, u32[]{:S(2)}, u32[]{:S(2)}) %collective-permute-start.2) | collective-permute-done | bytes 262176 | tf_op jit(solution)/shard_map/ppermute | solution.py:32
  37.7 4.4 %collective-permute-start.3 = (bf16[8,128,128]{2,1,0:T(8,128)(2,1)S(1)}, bf16[8,128,128]{2,1,0:T(8,128)(2,1)S(1)}, u32[]{:S(2)}, u32[]{:S(2)}) collective-permute-start(bf16[8,128,128]{2,1,0:T(8,128)(2,1)S(1)} %collective-permute-done.2), channel_id=1, source_target_pairs={{0,8},{8,16},{16,24},{24,32},{32,40},{40,48},{48,56},{56,64},{64,7... | collective-permute-start | bytes 786440 | tf_op jit(solution)/shard_map/ppermute | solution.py:32
  42.8 4.8 %collective-permute-done.3 = bf16[8,128,128]{2,1,0:T(8,128)(2,1)S(1)} collective-permute-done((bf16[8,128,128]{2,1,0:T(8,128)(2,1)S(1)}, bf16[8,128,128]{2,1,0:T(8,128)(2,1)S(1)}, u32[]{:S(2)}, u32[]{:S(2)}) %collective-permute-start.3) | collective-permute-done | bytes 262176 | tf_op jit(solution)/shard_map/ppermute | solution.py:32
  47.8 6.2 %collective-permute-start.4 = (bf16[8,128,128]{2,1,0:T(8,128)(2,1)S(1)}, bf16[8,128,128]{2,1,0:T(8,128)(2,1)S(1)}, u32[]{:S(2)}, u32[]{:S(2)}) collective-permute-start(bf16[8,128,128]{2,1,0:T(8,128)(2,1)S(1)} %fusion.37), channel_id=1, source_target_pairs={{0,16},{8,24},{16,32},{24,40},{32,48},{40,56},{48,64},{56,72},{64,... | collective-permute-start | bytes 786440 | tf_op jit(solution)/shard_map/ppermute | solution.py:32
  54.0 10.5 %collective-permute-done.4 = bf16[8,128,128]{2,1,0:T(8,128)(2,1)S(1)} collective-permute-done((bf16[8,128,128]{2,1,0:T(8,128)(2,1)S(1)}, bf16[8,128,128]{2,1,0:T(8,128)(2,1)S(1)}, u32[]{:S(2)}, u32[]{:S(2)}) %collective-permute-start.4) | collective-permute-done | bytes 262176 | tf_op jit(solution)/shard_map/ppermute | solution.py:32
  64.8 9.3 %collective-permute-start.5 = (bf16[8,128,128]{2,1,0:T(8,128)(2,1)S(1)}, bf16[8,128,128]{2,1,0:T(8,128)(2,1)S(1)}, u32[]{:S(2)}, u32[]{:S(2)}) collective-permute-start(bf16[8,128,128]{2,1,0:T(8,128)(2,1)S(1)} %fusion.64), channel_id=1, source_target_pairs={{0,32},{8,40},{16,48},{24,56},{32,64},{40,72},{48,80},{56,88},{64,... | collective-permute-start | bytes 786440 | tf_op jit(solution)/shard_map/ppermute | solution.py:32
  74.7 10.5 %collective-permute-done.5 = bf16[8,128,128]{2,1,0:T(8,128)(2,1)S(1)} collective-permute-done((bf16[8,128,128]{2,1,0:T(8,128)(2,1)S(1)}, bf16[8,128,128]{2,1,0:T(8,128)(2,1)S(1)}, u32[]{:S(2)}, u32[]{:S(2)}) %collective-permute-start.5) | collective-permute-done | bytes 262176 | tf_op jit(solution)/shard_map/ppermute | solution.py:32
  86.2 6.8 %collective-permute-start.6 = (bf16[8,128,128]{2,1,0:T(8,128)(2,1)}, bf16[8,128,128]{2,1,0:T(8,128)(2,1)}, u32[]{:S(2)}, u32[]{:S(2)}) collective-permute-start(bf16[8,128,128]{2,1,0:T(8,128)(2,1)} %fusion.43), channel_id=1, source_target_pairs={{0,64},{8,72},{16,80},{24,88},{32,96},{40,104},{48,112},{56,120},{... | collective-permute-start | bytes 786440 | tf_op jit(solution)/shard_map/ppermute | solution.py:32
  97.5 6.0 %collective-permute-done.6 = bf16[8,128,128]{2,1,0:T(8,128)(2,1)} collective-permute-done((bf16[8,128,128]{2,1,0:T(8,128)(2,1)}, bf16[8,128,128]{2,1,0:T(8,128)(2,1)}, u32[]{:S(2)}, u32[]{:S(2)}) %collective-permute-start.6) | collective-permute-done | bytes 262176 | tf_op jit(solution)/shard_map/ppermute | solution.py:32
  109.0 3.1 convolution_bitcast_fusion.1
  113.4 4.0 %multiply_reduce_fusion = (f32[128,16]{0,1:T(8,128)S(1)}, f32[128,16,128]{0,2,1:T(8,128)S(1)}) fusion(f32[128,16,128]{0,2,1:T(8,128)} %convolution_bitcast_fusion.1, f32[128,16]{0,1:T(8,128)S(1)} %get-tuple-element.26, f32[16,128,128]{2,1,0:T(8,128)} %copy-done.2, f32[8,128,128]{2,1,0:T(8,128)S(1)} %get-tuple-element.15, ...), kind=kOutput, calls=%fused_computation.28 | convolution fusion | flops 405010432 | bytes 4735041 | tf_op jit(solution)/shard_map/ihd,hde->ihe/dot_general | solution.py:98
  137.0 8.6 %convolution_convert_fusion.3 = bf16[64,3072]{1,0:T(8,128)(2,1)S(1)} fusion(bf16[2048,3072]{0,1:T(8,128)(2,1)} %all-gather.3.cloned.1.call-done, bf16[32,2048]{1,0:T(8,128)(2,1)} %get-tuple-element.21, bf16[32,2048]{1,0:T(8,128)(2,1)} %get-tuple-element.20), kind=kOutput, calls=%fused_computation.8 | convolution fusion | flops 806027264 | bytes 13238272 | tf_op jit(solution)/shard_map/dot_general | solution.py:140
  146.4 4.3 %all-to-all-start.1 = ((bf16[2,4,8,3072]{3,2,0,1:T(8,128)(2,1)}), bf16[2,4,8,3072]{3,2,0,1:T(8,128)(2,1)}, u32[]{:S(2)}, u32[]{:S(2)}) async-start(bf16[2,4,8,3072]{3,2,0,1:T(8,128)(2,1)} %copy.91), calls=%async_computation.1 | async-start | bytes 786432 | tf_op jit(solution)/shard_map/all_to_all | solution.py:142
  152.2 7.5 %all-to-all-done.1 = bf16[2,4,8,3072]{3,2,0,1:T(8,128)(2,1)} async-done(((bf16[2,4,8,3072]{3,2,0,1:T(8,128)(2,1)}), bf16[2,4,8,3072]{3,2,0,1:T(8,128)(2,1)}, u32[]{:S(2)}, u32[]{:S(2)}) %all-to-all-start.1) | async-done | bytes 393248 | tf_op jit(solution)/shard_map/all_to_all | solution.py:142
  172.7 42.0 %all-gather.5.cloned.1.call-done = bf16[16,8,6144]{2,1,0:T(8,128)(2,1)} async-done(((bf16[1,8,6144]{2,1,0:T(8,128)(2,1)}), bf16[16,8,6144]{2,1,0:T(8,128)(2,1)}) %all-gather.5.cloned.1.call-update) | async-done | bytes 1572880 | tf_op jit(solution)/shard_map/all_gather | solution.py:161
  216.0 8.0 %convolution_convert_fusion.2 = bf16[256,3072]{1,0:T(8,128)(2,1)S(1)} fusion(bf16[2048,3072]{0,1:T(8,128)(2,1)} %all-gather.3.cloned.1.call-done, bf16[128,2048]{1,0:T(8,128)(2,1)S(1)} %get-tuple-element.13, bf16[128,2048]{1,0:T(8,128)(2,1)S(1)} %get-tuple-element.12), kind=kOutput, calls=%fused_computation.2 | convolution fusion | flops 3224109056 | bytes 15204352 | tf_op jit(solution)/shard_map/dot_general | solution.py:140
  225.4 4.6 %all-to-all-start = ((bf16[2,4,32,3072]{3,2,0,1:T(8,128)(2,1)}), bf16[2,4,32,3072]{3,2,0,1:T(8,128)(2,1)}, u32[]{:S(2)}, u32[]{:S(2)}) async-start(bf16[2,4,32,3072]{3,2,0,1:T(8,128)(2,1)} %copy.85), calls=%async_computation | async-start | bytes 3145728 | tf_op jit(solution)/shard_map/all_to_all | solution.py:142
  237.1 9.4 %convolution_convert_fusion = bf16[256,6144]{1,0:T(8,128)(2,1)} fusion(bf16[1,288,6144]{2,1,0:T(8,128)(2,1)S(1)} %copy-done, f32[256,288]{0,1:T(8,128)} %fusion.1, bf16[256,6144]{1,0:T(8,128)(2,1)} %bitcast.108, bf16[1,6144,288]{1,2,0:T(8,128)(2,1)} %param.25), kind=kOutput, calls=%fused_computation | convolution fusion | flops 1813954560 | bytes 13664256 | tf_op jit(solution)/shard_map/dot_general | solution.py:168
  253.9 5.3 %dynamic-slice_reduce_fusion.1 = (bf16[32,16,192]{2,1,0:T(8,128)(2,1)}, bf16[32,16,192]{2,1,0:T(8,128)(2,1)}) fusion(bf16[32,16,2,192]{3,2,1,0:T(2,128)(2,1)} %reshape.296, s32[]{:T(128)S(6)} %select_n.151, s32[]{:T(128)S(6)} %select_n.152), kind=kLoop, calls=%fused_computation.63 | loop fusion | bytes 786440 | tf_op jit(solution)/shard_map/jit(dynamic_index_in_dim)/dynamic_slice | solution.py:134
  268.2 3.4 %fusion.5 = bf16[16,8,6144]{2,1,0:T(8,128)(2,1)} fusion(bf16[16,8,6144]{2,1,0:T(8,128)(2,1)} %collective-permute-done.14, bf16[16,2,8,6144]{3,2,1,0:T(8,128)(2,1)} %bitcast.106, s32[]{:T(128)S(6)} %select_n.151), kind=kLoop, calls=%fused_computation.11 | loop fusion | flops 3145728 | bytes 4718596 | tf_op jit(solution)/shard_map/convert_element_type | solution.py:173
  271.7 5.0 %all-to-all-start.2 = ((bf16[16,8,6144]{2,1,0:T(8,128)(2,1)}), bf16[16,8,6144]{2,1,0:T(8,128)(2,1)}, u32[]{:S(2)}, u32[]{:S(2)}) async-start(bf16[16,8,6144]{2,1,0:T(8,128)(2,1)} %fusion.5), calls=%async_computation.2 | async-start | bytes 3145728 | tf_op jit(solution)/shard_map/all_to_all | solution.py:173
  289.1 12.9 %all-to-all-done.2 = bf16[16,8,6144]{2,1,0:T(8,128)(2,1)} async-done(((bf16[16,8,6144]{2,1,0:T(8,128)(2,1)}), bf16[16,8,6144]{2,1,0:T(8,128)(2,1)}, u32[]{:S(2)}, u32[]{:S(2)}) %all-to-all-start.2) | async-done | bytes 1572896 | tf_op jit(solution)/shard_map/all_to_all | solution.py:173
  (135 shorter events, 101.4 us)
Async XLA Ops:
  7.2 229.9 %copy-start = (bf16[1,288,6144]{2,1,0:T(8,128)(2,1)S(1)}, bf16[1,288,6144]{2,1,0:T(8,128)(2,1)}, u32[]{:S(2)}) copy-start(bf16[1,288,6144]{2,1,0:T(8,128)(2,1)} %param.27) | copy-start | bytes 10616836
  7.2 129.8 %all-gather.3.cloned.1.call-start = ((), (), s32[]{:S(2)}) async-start(), calls=%async_computation.3 | async-start | bytes 13369344 | tf_op jit(solution)/shard_map/all_gather | solution.py:124
  15.1 3.0 collective-permute-start.1
  15.8 58.3 %copy-start.13 = (s32[128,2]{0,1:T(2,128)S(1)}, s32[128,2]{0,1:T(2,128)}, u32[]{:S(2)}) copy-start(s32[128,2]{0,1:T(2,128)} %param.23) | copy-start | bytes 3076
  21.8 15.9 %collective-permute-start.2 = (bf16[8,128,128]{2,1,0:T(8,128)(2,1)S(1)}, bf16[8,128,128]{2,1,0:T(8,128)(2,1)S(1)}, u32[]{:S(2)}, u32[]{:S(2)}) collective-permute-start(bf16[8,128,128]{2,1,0:T(8,128)(2,1)S(1)} %fusion.28), channel_id=1, source_target_pairs={{0,8},{8,16},{16,24},{24,32},{32,40},{40,48},{48,56},{56,64},{64,7... | collective-permute-start | bytes 786440 | tf_op jit(solution)/shard_map/ppermute | solution.py:32
  37.7 9.9 %collective-permute-start.3 = (bf16[8,128,128]{2,1,0:T(8,128)(2,1)S(1)}, bf16[8,128,128]{2,1,0:T(8,128)(2,1)S(1)}, u32[]{:S(2)}, u32[]{:S(2)}) collective-permute-start(bf16[8,128,128]{2,1,0:T(8,128)(2,1)S(1)} %collective-permute-done.2), channel_id=1, source_target_pairs={{0,8},{8,16},{16,24},{24,32},{32,40},{40,48},{48,56},{56,64},{64,7... | collective-permute-start | bytes 786440 | tf_op jit(solution)/shard_map/ppermute | solution.py:32
  42.8 50.2 %copy-start.8 = (f32[8]{0:T(128)}, f32[8]{0:T(128)S(1)}, u32[]{:S(2)}) copy-start(f32[8]{0:T(128)S(1)} %get-tuple-element.29) | copy-start | bytes 100
  42.8 50.2 %copy-start.11 = (f32[8]{0:T(128)}, f32[8]{0:T(128)S(1)}, u32[]{:S(2)}) copy-start(f32[8]{0:T(128)S(1)} %get-tuple-element.28) | copy-start | bytes 100
  47.8 16.7 %collective-permute-start.4 = (bf16[8,128,128]{2,1,0:T(8,128)(2,1)S(1)}, bf16[8,128,128]{2,1,0:T(8,128)(2,1)S(1)}, u32[]{:S(2)}, u32[]{:S(2)}) collective-permute-start(bf16[8,128,128]{2,1,0:T(8,128)(2,1)S(1)} %fusion.37), channel_id=1, source_target_pairs={{0,16},{8,24},{16,32},{24,40},{32,48},{40,56},{48,64},{56,72},{64,... | collective-permute-start | bytes 786440 | tf_op jit(solution)/shard_map/ppermute | solution.py:32
  64.8 20.4 %collective-permute-start.5 = (bf16[8,128,128]{2,1,0:T(8,128)(2,1)S(1)}, bf16[8,128,128]{2,1,0:T(8,128)(2,1)S(1)}, u32[]{:S(2)}, u32[]{:S(2)}) collective-permute-start(bf16[8,128,128]{2,1,0:T(8,128)(2,1)S(1)} %fusion.64), channel_id=1, source_target_pairs={{0,32},{8,40},{16,48},{24,56},{32,64},{40,72},{48,80},{56,88},{64,... | collective-permute-start | bytes 786440 | tf_op jit(solution)/shard_map/ppermute | solution.py:32
  86.2 17.3 %collective-permute-start.6 = (bf16[8,128,128]{2,1,0:T(8,128)(2,1)}, bf16[8,128,128]{2,1,0:T(8,128)(2,1)}, u32[]{:S(2)}, u32[]{:S(2)}) collective-permute-start(bf16[8,128,128]{2,1,0:T(8,128)(2,1)} %fusion.43), channel_id=1, source_target_pairs={{0,64},{8,72},{16,80},{24,88},{32,96},{40,104},{48,112},{56,120},{... | collective-permute-start | bytes 786440 | tf_op jit(solution)/shard_map/ppermute | solution.py:32
  106.0 6.1 %collective-permute-start.7 = (f32[8,128,128]{2,1,0:T(8,128)}, f32[8,128,128]{2,1,0:T(8,128)}, u32[]{:S(2)}, u32[]{:S(2)}) collective-permute-start(f32[8,128,128]{2,1,0:T(8,128)} %multiply_add_fusion), channel_id=1, source_target_pairs={{0,4},{4,0},{1,5},{5,1},{2,6},{6,2},{3,7},{7,3},{8,12},{12,8},{9,1... | collective-permute-start | bytes 1572872 | tf_op jit(solution)/shard_map/ppermute | solution.py:11
  125.1 10.2 %collective-permute-start.11 = (bf16[32,2048]{1,0:T(8,128)(2,1)}, bf16[32,2048]{1,0:T(8,128)(2,1)}, u32[]{:S(2)}, u32[]{:S(2)}) collective-permute-start(bf16[32,2048]{1,0:T(8,128)(2,1)} %convolution_convert_fusion.4), channel_id=1, source_target_pairs={{0,4},{4,0},{1,5},{5,1},{2,6},{6,2},{3,7},{7,3},{8,12},{12,8},{9,1... | collective-permute-start | bytes 393224 | tf_op jit(solution)/shard_map/ppermute | solution.py:11
  133.8 16.9 %collective-permute-start.10 = (bf16[8,3072]{1,0:T(8,128)(2,1)}, bf16[8,3072]{1,0:T(8,128)(2,1)}, u32[]{:S(2)}, u32[]{:S(2)}) collective-permute-start(bf16[8,3072]{1,0:T(8,128)(2,1)} %reshape.309), channel_id=1, source_target_pairs={{0,4},{4,0},{1,5},{5,1},{2,6},{6,2},{3,7},{7,3},{8,12},{12,8},{9,1... | collective-permute-start | bytes 147464 | tf_op jit(solution)/shard_map/ppermute | solution.py:11
  146.4 13.2 %all-to-all-start.1 = ((bf16[2,4,8,3072]{3,2,0,1:T(8,128)(2,1)}), bf16[2,4,8,3072]{3,2,0,1:T(8,128)(2,1)}, u32[]{:S(2)}, u32[]{:S(2)}) async-start(bf16[2,4,8,3072]{3,2,0,1:T(8,128)(2,1)} %copy.91), calls=%async_computation.1 | async-start | bytes 786432 | tf_op jit(solution)/shard_map/all_to_all | solution.py:142
  150.7 64.0 %all-gather.5.cloned.1.call-start = ((), (), s32[]{:S(2)}) async-start(), calls=%async_computation.4 | async-start | bytes 1671168 | tf_op jit(solution)/shard_map/all_gather | solution.py:161
  161.6 1.3 collective-permute-start.12
  172.4 42.3 %collective-permute-start.8 = (bf16[128,2048]{1,0:T(8,128)(2,1)}, bf16[128,2048]{1,0:T(8,128)(2,1)}, u32[]{:S(2)}, u32[]{:S(2)}) collective-permute-start(bf16[128,2048]{1,0:T(8,128)(2,1)} %copy-done.3), channel_id=1, source_target_pairs={{0,4},{4,0},{1,5},{5,1},{2,6},{6,2},{3,7},{7,3},{8,12},{12,8},{9,1... | collective-permute-start | bytes 1572872 | tf_op jit(solution)/shard_map/ppermute | solution.py:11
  214.7 15.3 %collective-permute-start.13 = (bf16[16,8,6144]{2,1,0:T(8,128)(2,1)}, bf16[16,8,6144]{2,1,0:T(8,128)(2,1)}, u32[]{:S(2)}, u32[]{:S(2)}) collective-permute-start(bf16[16,8,6144]{2,1,0:T(8,128)(2,1)} %all-gather.5.cloned.1.call-done), channel_id=1, source_target_pairs={{0,4},{4,0},{1,5},{5,1},{2,6},{6,2},{3,7},{7,3},{8,12},{12,8},{9,1... | collective-permute-start | bytes 4718600 | tf_op jit(solution)/shard_map/ppermute | solution.py:11
  225.4 40.1 %all-to-all-start = ((bf16[2,4,32,3072]{3,2,0,1:T(8,128)(2,1)}), bf16[2,4,32,3072]{3,2,0,1:T(8,128)(2,1)}, u32[]{:S(2)}, u32[]{:S(2)}) async-start(bf16[2,4,32,3072]{3,2,0,1:T(8,128)(2,1)} %copy.85), calls=%async_computation | async-start | bytes 3145728 | tf_op jit(solution)/shard_map/all_to_all | solution.py:142
  249.2 19.0 %collective-permute-start.14 = (bf16[16,8,6144]{2,1,0:T(8,128)(2,1)}, bf16[16,8,6144]{2,1,0:T(8,128)(2,1)}, u32[]{:S(2)}, u32[]{:S(2)}) collective-permute-start(bf16[16,8,6144]{2,1,0:T(8,128)(2,1)} %dynamic-slice_bitcast_fusion), channel_id=1, source_target_pairs={{0,4},{4,0},{1,5},{5,1},{2,6},{6,2},{3,7},{7,3},{8,12},{12,8},{9,1... | collective-permute-start | bytes 4718600 | tf_op jit(solution)/shard_map/ppermute | solution.py:11
  261.1 2.6 collective-permute-start
  271.7 30.4 %all-to-all-start.2 = ((bf16[16,8,6144]{2,1,0:T(8,128)(2,1)}), bf16[16,8,6144]{2,1,0:T(8,128)(2,1)}, u32[]{:S(2)}, u32[]{:S(2)}) async-start(bf16[16,8,6144]{2,1,0:T(8,128)(2,1)} %fusion.5), calls=%async_computation.2 | async-start | bytes 3145728 | tf_op jit(solution)/shard_map/all_to_all | solution.py:173
  278.1 1.5 collective-permute-start.9
  (14 other events, 196.6 us)
Sparse Core Ops, SparseCore 0:
  10.2 105.6 all-gather.2
  172.6 42.1 all-gather.4
